TPU v7x, 256 devices: a whole 4x4x8 slice. The times are simulated.
256 devices in a mesh: tm: 32 (over y, x, core), freq: 8 (over z).
Axes of the slice: x: 4, y: 4, z: 8, core: 2. Of those that a mesh axis runs over, the one named last changes fastest.
Arguments:
- increments: float32 [4096, 4, 128], P('tm'), may hold values from -6 to 6
- projections: float32 [128, 3, 4096], P(None, None, 'freq'), may hold values from -0.5 to 0.5
- phases: float32 [3, 4096], P(None, 'freq'), may hold values from -3.140625 to 3.140625
- groups: int32 [4], replicated, may hold values from 0 to 1, as said below
Outputs:
- grad_increments: float32 [4096, 4, 128], P(('tm', 'freq'))
- grad_projections: float32 [128, 3, 4096], P('tm', None, 'freq')
Inputs may be any that keep to these rules, and one draw needn't show every extreme that they name: `groups`: exactly 2 sequences have 1.
All inputs are finite; a program needn't handle non-finite values.
Results may differ from a plain program's by a relative error of at most 0.0003.
Values sent between devices are 32-bit elements; how exact they have to be, the bound alone decides.
A program may use at most 64 MiB of HBM per device.

v0:
```python
import math

import jax
import jax.numpy as jnp
from jax import lax
from jax.sharding import PartitionSpec as P

highest = lax.Precision.HIGHEST


def prefix(part, axis, combine, identity, reverse):
    count = lax.axis_size(axis)
    place = lax.axis_index(axis)
    ahead = count - 1 - place if reverse else place
    gathered = lax.all_gather(part, axis)
    state = jnp.zeros_like(part) + jnp.asarray(identity, part.dtype)

    def one(step, state):
        source = count - 1 - step if reverse else step
        return combine(state, lax.dynamic_index_in_dim(gathered, source, 0, False))

    return lax.fori_loop(0, ahead, one, state)


def add_terms(early, late):
    return early + late


def carry_forward(values):
    return prefix(values, "tm", add_terms, jnp.zeros_like(values), False)


def carry_backward(values):
    return prefix(values, "tm", add_terms, jnp.zeros_like(values), True)


def global_gaps(totals, set_weight):
    stacked = jnp.stack([jnp.sum(set_weight * total, axis=0) for total in totals], axis=0)
    return lax.psum(stacked, "tm")


def tiled_sum(values, forward):
    steps, batch, width = values.shape
    tile = min(128, steps)
    count = steps // tile
    row_ids = lax.broadcasted_iota(jnp.int32, (tile, tile), 0)
    col_ids = lax.broadcasted_iota(jnp.int32, (tile, tile), 1)
    if forward:
        tri_mask = (col_ids < row_ids).astype(jnp.float32)
    else:
        tri_mask = (col_ids > row_ids).astype(jnp.float32)
    blocks = values.reshape(count, tile, batch, width)
    inner = jnp.einsum("ts,nsbf->ntbf", tri_mask, blocks, precision=highest)
    block_sums = jnp.sum(blocks, axis=1)
    running = jnp.cumsum(block_sums, axis=0)
    if forward:
        outer = running - block_sums
    else:
        outer = running - running
    return (inner + outer[:, None]).reshape(steps, batch, width)


def on_device(increments, projections, phases, groups):
    steps, batch, chans = increments.shape
    length = steps * lax.axis_size("tm")
    amplitude = math.sqrt(2.0 / length)
    set_weight = jnp.where(groups == 1, 2.0 / batch, -2.0 / batch).astype(jnp.float32)[:, None]

    def before(values):
        return tiled_sum(values, True)

    def after(values):
        return tiled_sum(values, False)

    angles = [
        jnp.einsum("tbc,cf->tbf", increments, projections[:, degree, :], precision=highest)
        + phases[degree][None, None, :]
        for degree in range(3)
    ]
    waves = [amplitude * jnp.cos(angle) for angle in angles]
    entry1 = carry_forward(jnp.sum(waves[0], axis=0))
    front1 = entry1[None] + before(waves[0])
    term2 = front1 * waves[1]
    entry2 = carry_forward(jnp.sum(term2, axis=0))
    front2 = entry2[None] + before(term2)
    totals = (jnp.sum(waves[0], axis=0), jnp.sum(term2, axis=0), jnp.sum(front2 * waves[2], axis=0))
    gaps = global_gaps(totals, set_weight)
    seeds = [2.0 * set_weight * gaps[degree][None, :] for degree in range(3)]
    tail3 = carry_backward(jnp.sum(waves[2], axis=0))
    adjoint1 = seeds[1][None] + seeds[2][None] * (tail3[None] + after(waves[2]))
    product = adjoint1 * waves[1]
    tail2 = carry_backward(jnp.sum(product, axis=0))
    adjoint0 = seeds[0][None] + tail2[None] + after(product)
    directions = [adjoint0, adjoint1 * front1, seeds[2][None] * front2]
    slopes = [-amplitude * jnp.sin(angles[degree]) * directions[degree] for degree in range(3)]
    piece = increments
    grad_projections = lax.psum_scatter(
        jnp.stack(
            [jnp.einsum("tbc,tbf->cf", piece, slope, precision=highest) for slope in slopes], axis=1
        ),
        "tm",
        scatter_dimension=0,
        tiled=True,
    )
    result = jnp.zeros(
        (lax.axis_size("freq") * (steps // lax.axis_size("freq")), batch, chans), jnp.float32
    )
    for degree in range(3):
        piece = slopes[degree]
        result = result + jnp.einsum(
            "tbf,cf->tbc", piece, projections[:, degree, :], precision=highest
        )
    grad_increments = lax.psum_scatter(result, "freq", scatter_dimension=0, tiled=True)
    return (grad_increments, grad_projections)


def solution(mesh):
    placed = (P("tm", None, None), P(None, None, "freq"), P(None, "freq"), P())
    return jax.shard_map(
        on_device,
        mesh=mesh,
        in_specs=placed,
        out_specs=(P(("tm", "freq"), None, None), P("tm", None, "freq")),
        check_vma=False,
    )
```

profile of v0, /device:TPU:1, one launch (start us, length us, event | category | flops | bytes accessed | tf_op | source)
XLA Modules:
  0.0 423.6 jit_solution(12538549570355507986)
XLA Ops:
  8.7 6.3 %fusion.15 = (f32[4,512]{1,0:T(4,128)S(1)}, f32[128,4,512]{2,0,1:T(8,128)}) fusion(f32[512]{0:T(512)S(1)} %bitcast.158, f32[128,3,512]{2,0,1:T(8,128)} %param.13, f32[128,4,128]{2,1,0:T(4,128)} %param.12), kind=kOutput, calls=%fused_computation.37 | convolution fusion | flops 403437568 | bytes 1583104 | tf_op jit(solution)/shard_map/tbc,cf->tbf/dot_general | solution.py:76
  15.1 1.0 convolution_add_fusion.1
  16.1 1.0 convolution_add_fusion
  17.1 26.5 %all-gather.4 = f32[32,4,512]{2,1,0:T(4,128)S(1)} all-gather(f32[1,4,512]{2,1,0:T(4,128)S(1)} %bitcast.152), channel_id=2, replica_groups=mesh['tm'=32,'freq'=8] {'tm'}, dimensions={0}, use_global_device_ids=true | all-gather | bytes 270336 | tf_op jit(solution)/shard_map/all_gather | solution.py:15
  43.6 8.9 %fusion.22 = (f32[4,512]{1,0:T(4,128)S(1)}, f32[128,4,512]{2,0,1:T(8,128)S(1)}) fusion(f32[128,4,512]{2,0,1:T(8,128)S(1)} %convolution_add_fusion.1, f32[4,512]{1,0:T(4,128)S(1)} %sub.52, f32[128,4,512]{2,0,1:T(8,128)} %get-tuple-element.216, f32[4,512]{1,0:T(4,128)S(1)} %get-tuple-element.160), kind=kOutput, calls=%fused_computation.44 | convolution fusion | flops 404240384 | bytes 3170304 | tf_op jit(solution)/shard_map/ts,nsbf->ntbf/dot_general | solution.py:53
  52.5 27.1 %all-gather.5 = f32[32,4,512]{2,1,0:T(4,128)} all-gather(f32[1,4,512]{2,1,0:T(4,128)S(1)} %bitcast.153), channel_id=3, replica_groups=mesh['tm'=32,'freq'=8] {'tm'}, dimensions={0}, use_global_device_ids=true | all-gather | bytes 270336 | tf_op jit(solution)/shard_map/all_gather | solution.py:15
  80.4 8.7 %multiply_reduce_fusion = (f32[4,512]{1,0:T(4,128)S(1)}, f32[4,512]{1,0:T(4,128)S(1)}, f32[128,4,512]{2,0,1:T(8,128)}) fusion(f32[128,4,512]{2,0,1:T(8,128)S(1)} %convolution_add_fusion, f32[4,512]{1,0:T(4,128)S(1)} %sub.53, f32[128,4,512]{2,0,1:T(8,128)S(1)} %get-tuple-element.218, f32[128,4,512]{2,0,1:T(8,128)S(1)} %convolution_add_fusion.1, ...), kind=kOutput, calls=%fused_computation.33 | convolution fusion | flops 404762624 | bytes 4227072 | tf_op jit(solution)/shard_map/ts,nsbf->ntbf/dot_general | solution.py:53
  89.0 45.4 %all-gather.6 = f32[32,4,512]{2,1,0:T(4,128)} all-gather(f32[1,4,512]{2,1,0:T(4,128)S(1)} %bitcast.154), channel_id=4, replica_groups=mesh['tm'=32,'freq'=8] {'tm'}, dimensions={0}, use_global_device_ids=true | all-gather | bytes 270336 | tf_op jit(solution)/shard_map/all_gather | solution.py:15
  134.5 21.2 %while.46 = (s32[]{:T(128)}, f32[4,512]{1,0:T(4,128)S(1)}, s32[]{:T(128)}, f32[32,4,512]{2,1,0:T(4,128)}, s32[]{:T(128)}, /*index=5*/s32[]{:T(128)}, s32[]{:T(128)}, s32[]{:T(128)}) while((s32[]{:T(128)}, f32[4,512]{1,0:T(4,128)S(1)}, s32[]{:T(128)}, f32[32,4,512]{2,1,0:T(4,128)}, s32[]{:T(128)}, /*index=5*/s32[]{:T(128)}, s32[]{:T(128)}, ...), condition=%wide.region_13.14_spmd, body=%wide.region_12.13_spmd.sunk | while | flops 2054 | bytes 24719 | solution.py:22
  155.8 64.0 %psum.7 = f32[3,512]{1,0:T(4,128)S(1)} all-reduce(f32[3,512]{1,0:T(4,128)S(1)} %pad_maximum_fusion.1), channel_id=1, replica_groups=mesh['tm'=32,'freq'=8] {'tm'}, use_global_device_ids=true, to_apply=%region_10.11 | all-reduce | flops 1536 | bytes 12288 | tf_op jit(solution)/shard_map/psum | solution.py:39
  220.0 8.6 %fusion.24 = (f32[4,512]{1,0:T(4,128)S(1)}, f32[128,4,512]{2,0,1:T(8,128)}) fusion(f32[128,4,512]{2,0,1:T(8,128)S(1)} %convolution_add_fusion.1, f32[4,512]{1,0:T(4,128)S(1)} %sub.55, f32[128,4,512]{2,0,1:T(8,128)S(1)} %convolution_add_fusion, f32[4,512]{1,0:T(4,128)S(1)} %get-tuple-element.162, f32[4,512]{1,0:T(4,128)S(1)} %get-tuple-element.212, ...), kind=kOutput, calls=%fused_computation.45 | convolution fusion | flops 404764672 | bytes 3186688 | tf_op jit(solution)/shard_map/ts,nsbf->ntbf/dot_general | solution.py:53
  228.6 24.9 %all-gather.7 = f32[32,4,512]{2,1,0:T(4,128)} all-gather(f32[1,4,512]{2,1,0:T(4,128)S(1)} %bitcast.155), channel_id=5, replica_groups=mesh['tm'=32,'freq'=8] {'tm'}, dimensions={0}, use_global_device_ids=true | all-gather | bytes 270336 | tf_op jit(solution)/shard_map/all_gather | solution.py:15
  253.5 21.2 %while.47 = (s32[]{:T(128)}, f32[4,512]{1,0:T(4,128)S(1)}, s32[]{:T(128)}, f32[32,4,512]{2,1,0:T(4,128)}, s32[]{:T(128)}, /*index=5*/s32[]{:T(128)}, s32[]{:T(128)}, s32[]{:T(128)}) while((s32[]{:T(128)}, f32[4,512]{1,0:T(4,128)S(1)}, s32[]{:T(128)}, f32[32,4,512]{2,1,0:T(4,128)}, s32[]{:T(128)}, /*index=5*/s32[]{:T(128)}, s32[]{:T(128)}, ...), condition=%wide.region_16.17_spmd, body=%wide.region_15.16_spmd.sunk | while | flops 2054 | bytes 24719 | solution.py:22
  274.7 6.4 %convolution_bitcast_fusion.4 = f32[128,1,512]{0,2,1:T(8,128)S(1)} fusion(f32[128,4,512]{2,0,1:T(8,128)} %get-tuple-element.219, f32[128,4,512]{2,0,1:T(8,128)S(1)} %convolution_add_fusion, f32[4,512]{1,0:T(4,128)S(1)} %get-tuple-element.212, f32[128,4,128]{2,1,0:T(4,128)S(1)} %copy-done.2), kind=kOutput, calls=%fused_computation.26 | convolution fusion | flops 403439616 | bytes 2629632 | tf_op jit(solution)/shard_map/tbc,tbf->cf/dot_general | solution.py:99
  281.2 5.1 %convolution_bitcast_fusion.5 = f32[128,1,512]{0,2,1:T(8,128)S(1)} fusion(f32[128,4,128]{2,1,0:T(4,128)S(1)} %copy-done.2, f32[128,4,512]{2,0,1:T(8,128)S(1)} %copy-done, f32[128,4,512]{2,0,1:T(8,128)S(1)} %get-tuple-element.218, f32[128,4,512]{2,0,1:T(8,128)S(1)} %convolution_add_fusion.1), kind=kOutput, calls=%fused_computation.27 | convolution fusion | flops 403439616 | bytes 3670016 | tf_op jit(solution)/shard_map/tbc,tbf->cf/dot_general | solution.py:99
  286.3 7.9 %fusion.9 = f32[128,4,512]{2,0,1:T(8,128)S(1)} fusion(f32[128,4,512]{2,0,1:T(8,128)S(1)} %copy-done.3, f32[4,512]{1,0:T(4,128)S(1)} %sub.56, f32[4,512]{1,0:T(4,128)S(1)} %multiply_add_fusion, f32[128,4,512]{2,0,1:T(8,128)S(1)} %copy-done, f32[128,4,512]{2,0,1:T(8,128)S(1)} %convolution_add_fusion.1), kind=kOutput, calls=%fused_computation.20 | convolution fusion | flops 404242432 | bytes 4210688 | tf_op jit(solution)/shard_map/ts,nsbf->ntbf/dot_general | solution.py:53
  294.3 1.8 convolution_bitcast_fusion.6
  296.1 0.9 pad_maximum_fusion
  297.0 2.5 copy.30
  299.8 2.3 fusion.29
  302.2 5.4 %convolution_add_fusion.4 = f32[128,4,128]{2,0,1:T(8,128)S(1)} fusion(f32[128,4,128]{2,0,1:T(8,128)S(1)} %fusion.29, f32[128,3,512]{2,0,1:T(8,128)} %param.13, f32[128,4,512]{2,0,1:T(8,128)S(1)} %copy-done.1, f32[128,4,512]{2,0,1:T(8,128)S(1)} %get-tuple-element.218, f32[128,4,512]{2,0,1:T(8,128)S(1)} %convolution_add_fusion.1), kind=kOutput, calls=%fused_computation.30 | convolution fusion | flops 403505152 | bytes 3932160 | tf_op jit(solution)/shard_map/tbf,cf->tbc/dot_general | solution.py:110
  307.6 6.0 %convolution_add_fusion.3 = f32[128,4,128]{2,0,1:T(8,128)} fusion(f32[128,4,128]{2,0,1:T(8,128)S(1)} %convolution_add_fusion.4, f32[128,4,512]{2,0,1:T(8,128)S(1)} %copy-done.5, f32[128,4,512]{2,0,1:T(8,128)S(1)} %convolution_add_fusion, f32[4,512]{1,0:T(4,128)S(1)} %get-tuple-element.212, f32[128,3,512]{2,0,1:T(8,128)} %param.13), kind=kOutput, calls=%fused_computation.29 | convolution fusion | flops 403505152 | bytes 2891776 | tf_op jit(solution)/shard_map/tbf,cf->tbc/dot_general | solution.py:110
  315.6 97.8 %all-reduce.3.cloned.1.call-done = f32[128,3,512]{2,1,0:T(4,128)} async-done(((f32[128,3,512]{2,1,0:T(4,128)}), f32[128,3,512]{2,1,0:T(4,128)}) %all-reduce.3.cloned.1.call-update) | async-done | bytes 786448
  414.8 1.4 copy.31
  (107 shorter events, 47.8 us)
Async XLA Ops:
  8.0 0.7 copy-start.7
  8.0 405.4 %all-reduce.3.cloned.1.call-start = ((), (), s32[]{:S(2)}) async-start(), calls=%async_computation.2 | async-start | bytes 2097152
  8.7 6.4 %copy-start.2 = (f32[128,4,128]{2,1,0:T(4,128)S(1)}, f32[128,4,128]{2,1,0:T(4,128)}, u32[]{:S(2)}) copy-start(f32[128,4,128]{2,1,0:T(4,128)} %param.12) | copy-start | bytes 786436
  8.7 6.4 %copy-start.6 = (f32[128,3,512]{2,0,1:T(8,128)S(1)}, f32[128,3,512]{2,0,1:T(8,128)}, u32[]{:S(2)}) copy-start(f32[128,3,512]{2,0,1:T(8,128)} %param.13) | copy-start | bytes 2359300
  134.5 21.2 %copy-start.8 = (s32[4]{0:T(128)S(1)}, s32[4]{0:T(128)}, u32[]{:S(2)}) copy-start(s32[4]{0:T(128)} %param.15) | copy-start | bytes 52
  274.7 6.4 %copy-start = (f32[128,4,512]{2,0,1:T(8,128)S(1)}, f32[128,4,512]{2,0,1:T(8,128)}, u32[]{:S(2)}) copy-start(f32[128,4,512]{2,0,1:T(8,128)} %get-tuple-element.221) | copy-start | bytes 3145732
  281.1 5.2 %copy-start.3 = (f32[128,4,512]{2,0,1:T(8,128)S(1)}, f32[128,4,512]{2,0,1:T(8,128)}, u32[]{:S(2)}) copy-start(f32[128,4,512]{2,0,1:T(8,128)} %get-tuple-element.216) | copy-start | bytes 3145732
  294.2 1.8 copy-start.4
  299.6 115.2 %reduce-scatter.2.cloned.1.call-start = ((), (), s32[]{:S(2)}) async-start(), calls=%async_computation.1 | async-start | bytes 294912 | tf_op jit(solution)/shard_map/reduce_scatter | solution.py:113
  299.8 2.4 copy-start.1
  302.2 5.4 %copy-start.5 = (f32[128,4,512]{2,0,1:T(8,128)S(1)}, f32[128,4,512]{2,0,1:T(8,128)}, u32[]{:S(2)}) copy-start(f32[128,4,512]{2,0,1:T(8,128)} %get-tuple-element.219) | copy-start | bytes 3145732
  313.7 0.7 copy-start.9
Sparse Core Ops, SparseCore 0:
  299.7 113.6 all-reduce.2
Sparse Core Ops, SparseCore 1:
  313.8 30.2 reduce-scatter.1
where the time goes:
time: 428 us; the launch traced here: 424 us
  blocking collectives  188 us (44%)
  waiting for transfers between devices  97.8 us (23%)
  matrix products  69.5 us (16%)
  other arithmetic  44.3 us (10%)
  between operations  16.4 us (4%)
  local copies, waits for them, and re-layouts  7.24 us (2%)
    all_gather x4, blocking collectives, prefix(): gathered = lax.all_gather(part, axis)  124 us
    unnamed x3, waiting for transfers between devices  97.8 us
    psum x1, blocking collectives, global_gaps(): return lax.psum(stacked, 'tm')  64 us
    add x62, other arithmetic, add_terms(): return early + late  43.1 us
    dot_general x4, matrix products, tiled_sum(): inner = jnp.einsum('ts,nsbf->ntbf', tri_mask, blocks, precision=highest)  34.1 us
    dot_general x3, matrix products, on_device(): jnp.einsum('tbf,cf->tbc', piece, projections[:, degree, :], precision=hig...  13.8 us
    dot_general x3, matrix products, on_device(): jnp.einsum('tbc,tbf->cf', piece, slope, precision=highest)  13.3 us
  transfers between devices with their start and end apart: 2, of which 1 were waited for; matrix products, arithmetic and copies ran while one was open for 4% of the time, Pallas kernels for 0%

commit v1 on v0

v1 whole, which is shorter than its diff:
```python
import functools
import math

import jax
import jax.numpy as jnp
from jax import lax
from jax.experimental import pallas as pl
from jax.experimental.pallas import tpu as pltpu
from jax.sharding import PartitionSpec as P

MESH = pl.DeviceIdType.MESH
F32 = jnp.float32
BF16 = jnp.bfloat16
TURN = 1.0 / (2.0 * math.pi)

SIN_POLY = (3.14159264, -5.16771008, 2.55007752, -0.59829129, 0.07765766)
COS_POLY = (1.0, -4.93480214, 4.05870916, -1.335212, 0.23493731, -0.02439632)

GRIDS = {32: (4, 4), 8: (2, 2)}

W0, W1, W2, A01, A12, A012 = range(6)


def halves(value):
    high = value.astype(BF16)
    return high, (value - high.astype(F32)).astype(BF16)


def dot(left, right):
    return jnp.dot(left, right, preferred_element_type=F32)


def dot_nt(left, right):
    return lax.dot_general(left, right, (((1,), (1,)), ((), ())), preferred_element_type=F32)


def poly(coefs, z):
    value = coefs[-1] * z + coefs[-2]
    for coef in coefs[-3::-1]:
        value = value * z + coef
    return value


def join(early, late):
    return [
        early[W0] + late[W0],
        early[W1] + late[W1],
        early[W2] + late[W2],
        early[A01] + late[A01] + early[W0] * late[W1],
        early[A12] + late[A12] + early[W1] * late[W2],
        early[A012] + late[A012] + early[A01] * late[W2] + early[W0] * late[A12],
    ]


def masked(tiles, keep):
    return [tile * keep for tile in tiles]


def around(buffer, count, place):
    members = [[buffer[k, q] for q in range(6)] for k in range(count)]
    total = members[0]
    for k in range(1, count):
        total = join(total, members[k])
    before = masked(members[0], jnp.where(place > 0, 1.0, 0.0).astype(F32))
    for k in range(1, count - 1):
        before = join(before, masked(members[k], jnp.where(place > k, 1.0, 0.0).astype(F32)))
    after = masked(members[1], jnp.where(place < 1, 1.0, 0.0).astype(F32))
    for k in range(2, count):
        after = join(after, masked(members[k], jnp.where(place < k, 1.0, 0.0).astype(F32)))
    return before, after, total


def kernel(
    sizes, inc_ref, proj_ref, phase_ref, group_ref, gi_out, gp_out,
    xl, xt, pr, pn, yb, wb, whl, fb, sh, sl, tri,
    summ, summ_in, xbuf, ybuf, coef, coef_send,
    gp, gp_in, gs, r1, t1, r2, fin, fin_in, gi, gi_in,
    pair_send, pair_recv, x_send, x_recv, y_send, y_recv, u_send, u_recv, v_send, v_recv, z_send, z_recv,
):
    ny, nx, nz, length = sizes
    steps, batch, chans, width = 128, 4, 128, 512
    half = width // 2
    rows = steps * batch
    strip = chans // (nx * ny)
    part = steps // nz
    amplitude = math.sqrt(2.0 / length)
    root = math.sqrt(2.0 * amplitude)
    sin_poly = [root * a for a in SIN_POLY]
    cos_poly = [-root * a for a in COS_POLY]

    tm, z = lax.axis_index("tm"), lax.axis_index("freq")
    core = lax.rem(tm, 2)
    x = lax.rem(tm // 2, nx)
    y = tm // (2 * nx)
    other = 1 - core
    pair = (tm + 1 - 2 * core, z)

    def along_x(k):
        return (y * (2 * nx) + k * 2 + core, z)

    def along_y(k):
        return (k * (2 * nx) + x * 2 + core, z)

    u, v = other * x + core * y, other * y + core * x

    def along_u(k):
        return (other * (y * (2 * nx) + k * 2) + core * (k * (2 * nx) + x * 2) + core, z)

    def along_v(k):
        return (other * (k * (2 * nx) + x * 2) + core * (y * (2 * nx) + k * 2) + core, z)

    def next_of(place, d, count):
        return lax.rem(place + d, count)

    barrier = pltpu.get_barrier_semaphore()
    peers = [pair]
    peers += [along_x(next_of(x, d, nx)) for d in range(1, nx)]
    peers += [along_y(next_of(y, d, ny)) for d in range(1, ny)]
    peers += [(tm, next_of(z, d, nz)) for d in range(1, nz)]
    for peer in peers:
        pl.semaphore_signal(barrier, inc=1, device_id=peer, device_id_type=MESH)

    def remote(src, dst, send, recv, peer):
        copy = pltpu.make_async_remote_copy(
            src_ref=src, dst_ref=dst, send_sem=send, recv_sem=recv, device_id=peer, device_id_type=MESH
        )
        copy.start()
        return copy

    for b in range(batch):
        block = inc_ref[pl.ds(b, steps, stride=batch), :]
        x1 = block.astype(BF16)
        left = block - x1.astype(F32)
        x2 = left.astype(BF16)
        x3 = (left - x2.astype(F32)).astype(BF16)
        at = slice(b * steps, (b + 1) * steps)
        for k, piece in enumerate((x1, x2, x1, x2, x3, x1)):
            xl[at, k * chans : (k + 1) * chans] = piece
        flip = block.T
        high, low = halves(flip)
        xt[0:chans, at] = high
        xt[chans : 2 * chans, at] = low

    row = lax.broadcasted_iota(jnp.int32, (steps, steps), 0)
    col = lax.broadcasted_iota(jnp.int32, (steps, steps), 1)
    lower = jnp.where(col < row, 1.0, 0.0).astype(BF16)
    upper = jnp.where(col > row, 1.0, 0.0).astype(BF16)
    for k in range(2):
        tri[0:steps, k * steps : (k + 1) * steps] = lower
        tri[steps : 2 * steps, k * steps : (k + 1) * steps] = upper

    def split_projections(i, carry):
        m, h = i // 2, lax.rem(i, 2)
        at = pl.ds(pl.multiple_of(h * half, half), half)
        block = proj_ref[m, :, at]
        high, low = halves(block)
        pn[m, 0:chans, at] = high
        pn[m, chans : 2 * chans, at] = low
        block = block * TURN
        p1 = block.astype(BF16)
        left = block - p1.astype(F32)
        p2 = left.astype(BF16)
        p3 = (left - p2.astype(F32)).astype(BF16)
        for k, piece in enumerate((p1, p1, p2, p2, p1, p3)):
            pr[m, k * chans : (k + 1) * chans, at] = piece
        return carry

    lax.fori_loop(0, 6, split_projections, 0)

    for m in range(3):
        yb[m * rows : (m + 1) * rows, :] = dot(xl[...], pr[m])
        shift = phase_ref[m : m + 1, :] * TURN

        def waves(i, carry, m=m, shift=shift):
            at = pl.ds(pl.multiple_of(m * rows + i * 16, 16), 16)
            turns = yb[at, :] + shift
            f = turns - jnp.round(turns)
            f2 = f * f
            s = f * poly(sin_poly, f2)
            c = poly(cos_poly, f2)
            w = amplitude - s * s
            wb[at, :] = w
            yb[at, :] = s * c
            high, low = halves(w)
            b, t = i // 8, lax.rem(i, 8)
            start = pl.multiple_of(b * (2 * steps) + t * 16, 16)
            whl[m, pl.ds(start, 16), :] = high
            whl[m, pl.ds(start + steps, 16), :] = low
            return carry

        lax.fori_loop(0, rows // 16, waves, 0)

    def local_sums(h, carry):
        at = pl.ds(pl.multiple_of(h * half, half), half)

        def put(q, b, value):
            total = jnp.sum(value, axis=0, keepdims=True)
            for l in range(2):
                summ[h, q, l * batch + b : l * batch + b + 1, :] = total[:, l * 128 : (l + 1) * 128]

        for b in range(batch):
            here = slice(b * steps, (b + 1) * steps)
            pair_rows = slice(b * 2 * steps, (b + 1) * 2 * steps)
            w0 = wb[b * steps : (b + 1) * steps, at]
            w1 = wb[rows + b * steps : rows + (b + 1) * steps, at]
            w2 = wb[2 * rows + b * steps : 2 * rows + (b + 1) * steps, at]
            put(W0, b, w0)
            put(W1, b, w1)
            put(W2, b, w2)
            b0 = dot(tri[0:steps, :], whl[0, pair_rows, at])
            fb[0, here, at] = b0
            both = dot(tri[...], whl[1, pair_rows, at])
            fb[1, here, at] = both[0:steps]
            fb[2, here, at] = both[steps : 2 * steps]
            a2 = dot(tri[steps : 2 * steps, :], whl[2, pair_rows, at])
            fb[3, here, at] = a2
            p = b0 * w1
            put(A01, b, p)
            b01 = dot(tri[0:steps, :], jnp.concatenate(halves(p), axis=0))
            fb[4, here, at] = b01
            put(A012, b, b01 * w2)
            q = a2 * w1
            put(A12, b, q)
            fb[5, here, at] = dot(tri[steps : 2 * steps, :], jnp.concatenate(halves(q), axis=0))
        return carry

    lax.fori_loop(0, 2, local_sums, 0)

    pl.semaphore_wait(barrier, len(peers))
    copies = []
    copy = remote(summ.at[other], summ_in, pair_send.at[0], pair_recv.at[0], pair)
    copies.append(copy)
    copy.wait_recv()
    mine = [summ[core, q] for q in range(6)]
    theirs = [summ_in[q] for q in range(6)]
    first = jnp.where(core == 0, 1.0, 0.0).astype(F32)
    core0 = [a * first + b * (1.0 - first) for a, b in zip(mine, theirs)]
    core1 = [b * first + a * (1.0 - first) for a, b in zip(mine, theirs)]
    for q, tile in enumerate(join(core0, core1)):
        xbuf[x, q] = tile
    for d in range(1, nx):
        k = next_of(x, d, nx)
        copies.append(remote(xbuf.at[x], xbuf.at[x], x_send.at[k], x_recv.at[x], along_x(k)))
    for d in range(1, nx):
        k = next_of(x, d, nx)
        pltpu.make_async_copy(xbuf.at[k], xbuf.at[k], x_recv.at[k]).wait()
    before_x, after_x, total = around(xbuf, nx, x)
    for q, tile in enumerate(total):
        ybuf[y, q] = tile
    for d in range(1, ny):
        k = next_of(y, d, ny)
        copies.append(remote(ybuf.at[y], ybuf.at[y], y_send.at[k], y_recv.at[y], along_y(k)))
    for d in range(1, ny):
        k = next_of(y, d, ny)
        pltpu.make_async_copy(ybuf.at[k], ybuf.at[k], y_recv.at[k]).wait()
    before_y, after_y, total = around(ybuf, ny, y)
    before = join(before_y, before_x)
    after = join(after_x, after_y)
    middle = join(before, core0)
    tail = join(core1, after)

    sub = lax.broadcasted_iota(jnp.int32, (8, 128), 0)
    weight = jnp.zeros((8, 128), F32)
    for b in range(batch):
        sign = jnp.where(group_ref[b] == 1, 2.0 / batch, -2.0 / batch).astype(F32)
        weight = jnp.where(lax.rem(sub, batch) == b, sign, weight)
    seeds = []
    for q in (W0, A01, A012):
        product = weight * total[q]
        gaps = []
        for l in range(2):
            gap = product[l * batch : l * batch + 1]
            for b in range(1, batch):
                gap = gap + product[l * batch + b : l * batch + b + 1]
            gaps.append(jnp.broadcast_to(gap, (8, 128)))
        seeds.append(2.0 * weight * jnp.where(sub < batch, gaps[0], gaps[1]))

    def coefs(ahead, behind):
        tail2 = seeds[1] * behind[W1] + seeds[2] * behind[A12]
        return [seeds[0] + tail2, seeds[1] + seeds[2] * behind[W2], seeds[2], ahead[W0], ahead[A01]]

    of_core0, of_core1 = coefs(before, tail), coefs(middle, after)
    for k in range(5):
        coef_send[k] = of_core1[k] * first + of_core0[k] * (1.0 - first)
        coef[core, k] = of_core0[k] * first + of_core1[k] * (1.0 - first)
    copy = remote(coef_send, coef.at[core], pair_send.at[1], pair_recv.at[1], pair)
    copies.append(copy)
    copy.wait_recv()

    def slopes(h, carry):
        for l in range(2):
            at = pl.ds(pl.multiple_of(h * half + l * 128, 128), 128)
            for b in range(batch):
                line = slice(l * batch + b, l * batch + b + 1)
                c0, c1, s2, e1, e2 = [coef[h, k, line, :] for k in range(5)]
                for t in range(0, steps, 64):
                    r = b * steps + t
                    here = slice(r, r + 64)
                    b0, b1, a1, a2, b01, q = [fb[k, here, at] for k in range(6)]
                    values = (
                        yb[r : r + 64, at] * (c0 + c1 * a1 + s2 * q),
                        yb[rows + r : rows + r + 64, at] * ((c1 + s2 * a2) * (e1 + b0)),
                        yb[2 * rows + r : 2 * rows + r + 64, at] * (s2 * (e2 + e1 * b1 + b01)),
                    )
                    for m in range(3):
                        high, low = halves(values[m])
                        sh[m, here, at] = high
                        sl[m, here, at] = low
        return carry

    lax.fori_loop(0, 2, slopes, 0)

    for b in range(batch):
        here = slice(b * steps, (b + 1) * steps)
        total = jnp.zeros((steps, chans), F32)
        for m in range(3):
            wide = dot_nt(sh[m, here, :], pn[m])
            total = total + wide[:, 0:chans] + wide[:, chans : 2 * chans] + dot_nt(sl[m, here, :], pn[m, 0:chans, :])
        gi[b] = total
    gi_copies = []
    for d in range(nz - 1, 0, -1):
        k = next_of(z, d, nz)
        src = gi.at[:, pl.ds(pl.multiple_of(k * part, part), part), :]
        gi_copies.append(remote(src, gi_in.at[z], z_send.at[k], z_recv.at[z], (tm, k)))

    def frequency_gradient(h):
        at = pl.ds(pl.multiple_of(h * half, half), half)
        for m in range(3):
            wide = dot(xt[...], sh[m, :, at])
            low = dot(xt[0:chans, :], sl[m, :, at])
            gp[h, :, m * half : (m + 1) * half] = wide[0:chans] + wide[chans : 2 * chans] + low

    frequency_gradient(other)
    pair_copy = remote(gp.at[other], gp_in, pair_send.at[2], pair_recv.at[2], pair)
    copies.append(pair_copy)
    frequency_gradient(core)
    pair_copy.wait_recv()
    for iy in range(ny):
        for ix in range(nx):
            at = slice((iy * nx + ix) * strip, (iy * nx + ix + 1) * strip)
            tile = gp[core, at, :] + gp_in[at, :]
            gs[other * ix + core * iy, other * iy + core * ix] = tile
    for d in range(1, nx):
        k = next_of(u, d, nx)
        copies.append(remote(gs.at[k], r1.at[u], u_send.at[k], u_recv.at[u], along_u(k)))
    r1[u] = gs[u]
    for d in range(1, nx):
        k = next_of(u, d, nx)
        pltpu.make_async_copy(r1.at[k], r1.at[k], u_recv.at[k]).wait()
    for j in range(ny):
        tile = r1[0, j]
        for k in range(1, nx):
            tile = tile + r1[k, j]
        t1[j] = tile
    for d in range(1, ny):
        k = next_of(v, d, ny)
        copies.append(remote(t1.at[k], r2.at[v], v_send.at[k], v_recv.at[v], along_v(k)))
    r2[v] = t1[v]
    for d in range(1, ny):
        k = next_of(v, d, ny)
        pltpu.make_async_copy(r2.at[k], r2.at[k], v_recv.at[k]).wait()
    tile = r2[0]
    for k in range(1, ny):
        tile = tile + r2[k]
    keep = strip // 2
    fin[0] = tile
    fin[1] = jnp.concatenate([tile[keep:], tile[:keep]], axis=0)
    copy = remote(fin.at[other], fin_in, pair_send.at[3], pair_recv.at[3], pair)
    copies.append(copy)

    for d in range(1, nz):
        k = next_of(z, d, nz)
        pltpu.make_async_copy(gi_in.at[k], gi_in.at[k], z_recv.at[k]).wait()
    own = gi[:, pl.ds(pl.multiple_of(z * part, part), part), :]
    gi_in[z] = own
    total = gi_in[0]
    for k in range(1, nz):
        total = total + gi_in[k]
    for b in range(batch):
        gi_out[pl.ds(b, part, stride=batch), :] = total[b]

    copy.wait_recv()
    for m in range(3):
        lanes = slice(m * half, (m + 1) * half)
        gp_out[m, :, pl.ds(pl.multiple_of(core * half, half), half)] = fin[core, 0:keep, lanes]
        gp_out[m, :, pl.ds(pl.multiple_of(other * half, half), half)] = fin_in[0:keep, lanes]
    for copy in copies + gi_copies:
        copy.wait_send()


def on_device(sizes, increments, projections, phases, groups):
    ny, nx, nz, _ = sizes
    steps, batch, chans = increments.shape
    width = projections.shape[2]
    strip = chans // (nx * ny)
    part = steps // nz
    rows = steps * batch
    half = width // 2
    vmem = pl.BlockSpec(memory_space=pltpu.VMEM)
    dma = pltpu.SemaphoreType.DMA
    gi, gp = pl.pallas_call(
        functools.partial(kernel, sizes),
        out_shape=(
            jax.ShapeDtypeStruct((part * batch, chans), F32),
            jax.ShapeDtypeStruct((3, strip // 2, width), F32),
        ),
        in_specs=[vmem, vmem, vmem, pl.BlockSpec(memory_space=pltpu.SMEM)],
        out_specs=(vmem, vmem),
        scratch_shapes=[
            pltpu.VMEM((rows, 6 * chans), BF16),
            pltpu.VMEM((2 * chans, rows), BF16),
            pltpu.VMEM((3, 6 * chans, width), BF16),
            pltpu.VMEM((3, 2 * chans, width), BF16),
            pltpu.VMEM((3 * rows, width), F32),
            pltpu.VMEM((3 * rows, width), F32),
            pltpu.VMEM((3, 2 * rows, width), BF16),
            pltpu.VMEM((6, rows, width), F32),
            pltpu.VMEM((3, rows, width), BF16),
            pltpu.VMEM((3, rows, width), BF16),
            pltpu.VMEM((2 * steps, 2 * steps), BF16),
            pltpu.VMEM((2, 6, 8, 128), F32),
            pltpu.VMEM((6, 8, 128), F32),
            pltpu.VMEM((nx, 6, 8, 128), F32),
            pltpu.VMEM((ny, 6, 8, 128), F32),
            pltpu.VMEM((2, 5, 8, 128), F32),
            pltpu.VMEM((5, 8, 128), F32),
            pltpu.VMEM((2, chans, 3 * half), F32),
            pltpu.VMEM((chans, 3 * half), F32),
            pltpu.VMEM((nx, ny, strip, 3 * half), F32),
            pltpu.VMEM((nx, ny, strip, 3 * half), F32),
            pltpu.VMEM((ny, strip, 3 * half), F32),
            pltpu.VMEM((ny, strip, 3 * half), F32),
            pltpu.VMEM((2, strip, 3 * half), F32),
            pltpu.VMEM((strip, 3 * half), F32),
            pltpu.VMEM((batch, steps, chans), F32),
            pltpu.VMEM((nz, batch, part, chans), F32),
            dma((4,)), dma((4,)),
            dma((nx,)), dma((nx,)),
            dma((ny,)), dma((ny,)),
            dma((nx,)), dma((nx,)),
            dma((ny,)), dma((ny,)),
            dma((nz,)), dma((nz,)),
        ],
        compiler_params=pltpu.CompilerParams(
            collective_id=0, has_side_effects=True, vmem_limit_bytes=60 << 20
        ),
    )(
        increments.reshape(rows, chans),
        projections.transpose(1, 0, 2),
        phases,
        groups,
    )
    return gi.reshape(part, batch, chans), gp.transpose(1, 0, 2)


def solution(mesh):
    tm, nz = mesh.shape["tm"], mesh.shape["freq"]
    ny, nx = GRIDS[tm]
    placed = (P("tm", None, None), P(None, None, "freq"), P(None, "freq"), P())
    return jax.shard_map(
        functools.partial(on_device, (ny, nx, nz, 128 * tm)),
        mesh=mesh,
        in_specs=placed,
        out_specs=(P(("tm", "freq"), None, None), P("tm", None, "freq")),
        check_vma=False,
    )
```

time: 428 us -> 41.8 us (0.10)
  blocking collectives: 188 us -> 0 us
  waiting for transfers between devices: 97.8 us -> 0 us
  matrix products: 69.5 us -> 0 us
  other arithmetic: 44.3 us -> 0 us
  Pallas kernels: 0 us -> 39 us
  between operations: 16.4 us -> 0.65 us
  local copies, waits for them, and re-layouts: 7.24 us -> 1.99 us
    all_gather x4 -> x0, blocking collectives: 124 us -> none  [prefix(): gathered = lax.all_gather(part, axis)]
    unnamed x3 -> x0, waiting for transfers between devices: 97.8 us -> none
    dot_general x13 -> x0, matrix products: 69.5 us -> none  [the longest x4 34.1 us: tiled_sum(): inner = jnp.einsum('ts,nsbf->ntbf', tri_mask, blocks, precision=highest)]
    psum x1 -> x0, blocking collectives: 64 us -> none  [global_gaps(): return lax.psum(stacked, 'tm')]
    add x63 -> x0, other arithmetic: 43.2 us -> none  [the longest x62 43.1 us: add_terms(): return early + late]
    pallas_call x0 -> x1, Pallas kernels: none -> 39 us  [on_device(): pl.pallas_call(functools.partial(kernel, sizes), out_shape=(jax.ShapeDtyp...]
  transfers between devices with their start and end apart: 2 -> 0, of which waited for: 1 -> 0; matrix products, arithmetic and copies ran while one was open for 4% -> 0% of each run, Pallas kernels for 0% -> 0%
where the time goes in v1:
time: 41.8 us; the launch traced here: 41.7 us
  Pallas kernels  39 us (93%)
  local copies, waits for them, and re-layouts  1.99 us (5%)
  between operations  0.65 us (2%)
    pallas_call x1, Pallas kernels, on_device(): pl.pallas_call(functools.partial(kernel, sizes), out_shape=(jax.ShapeDtyp...  39 us
    unnamed x4, local copies, waits for them, and re-layouts  1.99 us

profile of v1, /device:TPU:1, one launch (start us, length us, event | category | flops | bytes accessed | tf_op | source)
XLA Modules:
  0.0 41.7 jit_solution(3797093314292655682)
XLA Ops:
  0.6 39.0 %shard_map.59 = (f32[64,128]{1,0:T(8,128)}, f32[3,4,512]{2,1,0:T(4,128)}) custom-call(f32[512,128]{1,0:T(8,128)} %bitcast.5, f32[3,128,512]{2,1,0:T(8,128)} %bitcast.4, f32[3,512]{1,0:T(4,128)} %phase_ref.1, s32[4]{0:T(128)} %group_ref.1), custom_call_target="tpu_custom_call" | custom-call | tf_op jit(solution)/shard_map/pallas_call | solution.py:401
  39.7 0.0 copy-start
  39.7 1.4 %copy.8 = f32[16,4,128]{2,1,0:T(4,128)} copy(f32[16,4,128]{2,1,0:T(4,128)} %bitcast.6) | data formatting | bytes 65536
  41.1 0.0 copy-done
  41.1 0.6 %copy.9 = f32[4,3,512]{2,0,1:T(4,128)} copy(f32[4,3,512]{2,0,1:T(4,128)S(1)} %bitcast.7) | data formatting | bytes 49152
Async XLA Ops:
  39.7 1.4 %copy-start = (f32[3,4,512]{2,1,0:T(4,128)S(1)}, f32[3,4,512]{2,1,0:T(4,128)}, u32[]{:S(2)}) copy-start(f32[3,4,512]{2,1,0:T(4,128)} %get-tuple-element.5) | copy-start | bytes 73732

commit v2 on v0

v2 whole, which is shorter than its diff:
```python
import functools
import math

import jax
import jax.numpy as jnp
from jax import lax
from jax.experimental import pallas as pl
from jax.experimental.pallas import tpu as pltpu
from jax.sharding import PartitionSpec as P

MESH = pl.DeviceIdType.MESH
F32 = jnp.float32
BF16 = jnp.bfloat16
TURN = 1.0 / (2.0 * math.pi)

SIN_POLY = (3.14159264, -5.16771008, 2.55007752, -0.59829129, 0.07765766)
COS_POLY = (1.0, -4.93480214, 4.05870916, -1.335212, 0.23493731, -0.02439632)

NY, NX, NZ = 4, 4, 8
CHIPS = NY * NX
STEPS, BATCH, CHANS, WIDTH = 128, 4, 128, 512
LENGTH = STEPS * CHIPS * 2
HALF = WIDTH // 2
ROWS = STEPS * BATCH
PART = STEPS // NZ
LEVELS = 3

W0, W1, W2, A01, A12, A012 = range(6)


def halves(value):
    high = value.astype(BF16)
    return high, (value - high.astype(F32)).astype(BF16)


def dot(left, right):
    return jnp.dot(left, right, preferred_element_type=F32)


def dot_nt(left, right):
    return lax.dot_general(left, right, (((1,), (1,)), ((), ())), preferred_element_type=F32)


def poly(coefs, z):
    value = coefs[-1] * z + coefs[-2]
    for coef in coefs[-3::-1]:
        value = value * z + coef
    return value


def join(early, late):
    return [
        early[W0] + late[W0],
        early[W1] + late[W1],
        early[W2] + late[W2],
        early[A01] + late[A01] + early[W0] * late[W1],
        early[A12] + late[A12] + early[W1] * late[W2],
        early[A012] + late[A012] + early[A01] * late[W2] + early[W0] * late[A12],
    ]


def join_front(early, late):
    return {W0: early[W0] + late[W0], A01: early[A01] + late[A01] + early[W0] * late[W1]}


def join_back(early, late):
    return {
        W1: early[W1] + late[W1],
        W2: early[W2] + late[W2],
        A12: early[A12] + late[A12] + early[W1] * late[W2],
    }


def flag(condition):
    return jnp.where(condition, 1.0, 0.0).astype(F32)


def kernel(
    inc_hbm, proj_hbm, phase_ref, group_ref, gi_out, gp_out,
    inc_ref, proj_ref, xl, xt, pr, pt, fz, wb, whl, fb, sh, sl, tri,
    summ, summ_in, chips, coef, coef_send, gp_pair, gp_own, gp_in, gp_recv, gi, gi_in,
    in_sem, pair_send, pair_recv, c_send, c_recv, u_send, u_recv, z_send, z_recv,
):
    amplitude = math.sqrt(2.0 / LENGTH)
    root = math.sqrt(2.0 * amplitude)
    sin_poly = [root * a for a in SIN_POLY]
    cos_poly = [-root * a for a in COS_POLY]

    loads = [pltpu.make_async_copy(inc_hbm, inc_ref, in_sem.at[0])]
    loads += [pltpu.make_async_copy(proj_hbm.at[m], proj_ref.at[m], in_sem.at[1 + m]) for m in range(LEVELS)]
    for load in loads:
        load.start()

    tm, z = lax.axis_index("tm"), lax.axis_index("freq")
    core, chip = lax.rem(tm, 2), tm // 2
    other = 1 - core
    pair = (tm + 1 - 2 * core, z)

    def chip_at(d):
        return lax.rem(chip + d, CHIPS)

    def z_at(d):
        return lax.rem(z + d, NZ)

    barrier = pltpu.get_barrier_semaphore()
    peers = [pair] + [(2 * chip_at(d) + core, z) for d in range(1, CHIPS)] + [(tm, z_at(d)) for d in range(1, NZ)]
    for peer in peers:
        pl.semaphore_signal(barrier, inc=1, device_id=peer, device_id_type=MESH)

    def remote(src, dst, send, recv, peer):
        return pltpu.make_async_remote_copy(
            src_ref=src, dst_ref=dst, send_sem=send, recv_sem=recv, device_id=peer, device_id_type=MESH
        )

    row = lax.broadcasted_iota(jnp.int32, (STEPS, STEPS), 0)
    col = lax.broadcasted_iota(jnp.int32, (STEPS, STEPS), 1)
    lower = jnp.where(col < row, 1.0, 0.0).astype(BF16)
    upper = jnp.where(col > row, 1.0, 0.0).astype(BF16)
    for k in range(2):
        tri[0:STEPS, k * STEPS : (k + 1) * STEPS] = lower
        tri[STEPS : 2 * STEPS, k * STEPS : (k + 1) * STEPS] = upper

    loads[0].wait()
    for b in range(BATCH):
        block = inc_ref[pl.ds(b, STEPS, stride=BATCH), :]
        x1 = block.astype(BF16)
        left = block - x1.astype(F32)
        x2 = left.astype(BF16)
        x3 = (left - x2.astype(F32)).astype(BF16)
        at = slice(b * STEPS, (b + 1) * STEPS)
        for k, piece in enumerate((x1, x2, x1, x2, x3, x1)):
            xl[at, k * CHANS : (k + 1) * CHANS] = piece

    for m in range(LEVELS):
        loads[1 + m].wait()

        def split_projection(i, carry, m=m):
            at = pl.ds(pl.multiple_of(i * HALF, HALF), HALF)
            block = proj_ref[m, :, at] * TURN
            p1 = block.astype(BF16)
            left = block - p1.astype(F32)
            p2 = left.astype(BF16)
            p3 = (left - p2.astype(F32)).astype(BF16)
            for k, piece in enumerate((p1, p1, p2, p2, p1, p3)):
                pr[m, k * CHANS : (k + 1) * CHANS, at] = piece
            return carry

        lax.fori_loop(0, 2, split_projection, 0)

    pair_summ = remote(summ.at[other], summ_in, pair_send.at[0], pair_recv.at[0], pair)

    def local_sums(i, carry):
        h = lax.rem(core + 1 + i, 2)
        at = pl.ds(pl.multiple_of(h * HALF, HALF), HALF)

        def put(q, b, total):
            for l in range(2):
                summ[h, q, l * BATCH + b : l * BATCH + b + 1, :] = total[:, l * 128 : (l + 1) * 128]

        for m in range(LEVELS):
            turns_all = dot(xl[...], pr[m, :, at])
            shift = phase_ref[m : m + 1, at] * TURN
            for b in range(BATCH):
                total = jnp.zeros((16, HALF), F32)
                for t in range(0, STEPS, 16):
                    r = b * STEPS + t
                    turns = turns_all[r : r + 16] + shift
                    f = turns - jnp.round(turns)
                    fz[m, r : r + 16, at] = f
                    s = f * poly(sin_poly, f * f)
                    w = amplitude - s * s
                    total = total + w
                    if m == 1:
                        wb[r : r + 16, at] = w
                    high, low = halves(w)
                    whl[m, 2 * b * STEPS + t : 2 * b * STEPS + t + 16, at] = high
                    whl[m, (2 * b + 1) * STEPS + t : (2 * b + 1) * STEPS + t + 16, at] = low
                put(m, b, jnp.sum(total, axis=0, keepdims=True))
        for b in range(BATCH):
            here = slice(b * STEPS, (b + 1) * STEPS)
            both = slice(2 * b * STEPS, 2 * (b + 1) * STEPS)
            b0 = dot(tri[0:STEPS, :], whl[0, both, at])
            a2 = dot(tri[STEPS : 2 * STEPS, :], whl[2, both, at])
            fb[0, here, at] = b0
            fb[3, here, at] = a2
            sums = [jnp.zeros((16, HALF), F32)] * 3
            for t in range(0, STEPS, 16):
                w1 = wb[b * STEPS + t : b * STEPS + t + 16, at]
                p, a = b0[t : t + 16] * w1, a2[t : t + 16]
                sums = [sums[0] + p, sums[1] + a * w1, sums[2] + a * p]
            for q, total in zip((A01, A12, A012), sums):
                put(q, b, jnp.sum(total, axis=0, keepdims=True))

        @pl.when(i == 0)
        def _():
            pl.semaphore_wait(barrier, len(peers))
            pair_summ.start()

        return carry

    lax.fori_loop(0, 2, local_sums, 0)

    pair_summ.wait_recv()
    mine = [summ[core, q] for q in range(6)]
    theirs = [summ_in[q] for q in range(6)]
    first = flag(core == 0)
    core0 = [a * first + b * (1.0 - first) for a, b in zip(mine, theirs)]
    core1 = [b * first + a * (1.0 - first) for a, b in zip(mine, theirs)]
    for q, tile in enumerate(join(core0, core1)):
        chips[chip, q] = tile
    chip_copies = []
    for d in range(1, CHIPS):
        k = chip_at(d)
        copy = remote(chips.at[chip], chips.at[chip], c_send.at[k], c_recv.at[chip], (2 * k + core, z))
        copy.start()
        chip_copies.append(copy)

    def scans(i, carry):
        at = pl.ds(pl.multiple_of(i * HALF, HALF), HALF)
        for b in range(BATCH):
            here = slice(b * STEPS, (b + 1) * STEPS)
            both = dot(tri[...], whl[1, 2 * b * STEPS : 2 * (b + 1) * STEPS, at])
            fb[1, here, at] = both[0:STEPS]
            fb[2, here, at] = both[STEPS : 2 * STEPS]
            w1 = wb[here, at]
            fb[4, here, at] = dot(tri[0:STEPS, :], jnp.concatenate(halves(fb[0, here, at] * w1), axis=0))
            fb[5, here, at] = dot(tri[STEPS : 2 * STEPS, :], jnp.concatenate(halves(fb[3, here, at] * w1), axis=0))
        return carry

    lax.fori_loop(0, 2, scans, 0)

    def sines(i, carry):
        at = pl.ds(pl.multiple_of(i * 16, 16), 16)
        for m in range(LEVELS):
            for l in range(0, WIDTH, HALF):
                f = fz[m, at, l : l + HALF]
                f2 = f * f
                fz[m, at, l : l + HALF] = f * poly(sin_poly, f2) * poly(cos_poly, f2)
        return carry

    lax.fori_loop(0, ROWS // 16, sines, 0)

    for h in range(2):
        for m in range(LEVELS):
            for l in range(2):
                lanes = slice(h * HALF + l * 128, h * HALF + (l + 1) * 128)
                high, low = halves(proj_ref[m, :, lanes].T)
                down = slice(m * HALF + l * 128, m * HALF + (l + 1) * 128)
                pt[h, down, 0:CHANS] = high
                pt[h, down, CHANS : 2 * CHANS] = low

    for order in range(2):
        place = lax.rem(row, 64)
        k = place // 4
        k = k + order * (1 - 2 * lax.rem(k, 2))
        channel = 8 * k + 4 * (row // 64) + lax.rem(place, 4)
        pick = jnp.where(col == channel, 1.0, 0.0).astype(BF16)
        for b in range(BATCH):
            at = slice(b * STEPS, (b + 1) * STEPS)
            high = dot_nt(pick, xl[at, 0:CHANS]).astype(BF16)
            low = dot_nt(pick, xl[at, CHANS : 2 * CHANS]).astype(BF16)
            for c in range(2):
                xt[order, c, 0:64, at] = high[64 * c : 64 * (c + 1)]
                xt[order, c, 64:128, at] = low[64 * c : 64 * (c + 1)]

    sub = lax.broadcasted_iota(jnp.int32, (8, 128), 0)
    weight = jnp.zeros((8, 128), F32)
    for b in range(BATCH):
        sign = jnp.where(group_ref[b] == 1, 2.0 / BATCH, -2.0 / BATCH).astype(F32)
        weight = jnp.where(lax.rem(sub, BATCH) == b, sign, weight)

    for d in range(1, CHIPS):
        k = chip_at(d)
        remote(chips.at[k], chips.at[k], c_send.at[k], c_recv.at[k], (2 * k + core, z)).wait_recv()
    members = [[chips[k, q] for q in range(6)] for k in range(CHIPS)]
    total = members[0]
    for k in range(1, CHIPS):
        total = join(total, members[k])
    zero = jnp.zeros((8, 128), F32)
    before = [zero] * 6
    for k in range(CHIPS - 1):
        keep = flag(chip > k)
        before = join_front(before, [tile * keep for tile in members[k]])
    after = [zero] * 6
    for k in range(1, CHIPS):
        keep = flag(chip < k)
        after = join_back(after, [tile * keep for tile in members[k]])
    middle = join_front(before, core0)
    tail = join_back(core1, after)

    seeds = []
    for q in (W0, A01, A012):
        product = weight * total[q]
        gaps = []
        for l in range(2):
            gap = product[l * BATCH : l * BATCH + 1]
            for b in range(1, BATCH):
                gap = gap + product[l * BATCH + b : l * BATCH + b + 1]
            gaps.append(jnp.broadcast_to(gap, (8, 128)))
        seeds.append(2.0 * weight * jnp.where(sub < BATCH, gaps[0], gaps[1]))

    def coefs(ahead, behind):
        tail2 = seeds[1] * behind[W1] + seeds[2] * behind[A12]
        return [seeds[0] + tail2, seeds[1] + seeds[2] * behind[W2], seeds[2], ahead[W0], ahead[A01]]

    of_core0, of_core1 = coefs(before, tail), coefs(middle, after)
    for k in range(5):
        coef_send[k] = of_core1[k] * first + of_core0[k] * (1.0 - first)
        coef[core, k] = of_core0[k] * first + of_core1[k] * (1.0 - first)
    pair_coef = remote(coef_send, coef.at[core], pair_send.at[1], pair_recv.at[1], pair)
    pair_coef.start()

    def slopes(h):
        for l in range(2):
            at = pl.ds(pl.multiple_of(h * HALF + l * 128, 128), 128)
            for b in range(BATCH):
                line = slice(l * BATCH + b, l * BATCH + b + 1)
                c0, c1, s2, e1, e2 = [coef[h, k, line, :] for k in range(5)]
                for t in range(0, STEPS, 64):
                    r = b * STEPS + t
                    here = slice(r, r + 64)
                    b0, b1, a1, a2, b01, q = [fb[k, here, at] for k in range(6)]
                    values = (
                        fz[0, here, at] * (c0 + c1 * a1 + s2 * q),
                        fz[1, here, at] * ((c1 + s2 * a2) * (e1 + b0)),
                        fz[2, here, at] * (s2 * (e2 + e1 * b1 + b01)),
                    )
                    for m in range(LEVELS):
                        high, low = halves(values[m])
                        lanes = slice(m * HALF + l * 128, m * HALF + (l + 1) * 128)
                        sh[h, here, lanes] = high
                        sl[h, here, lanes] = low

    def increments_part(h):
        wide = dot(sh[h], pt[h])
        return wide[:, 0:CHANS] + wide[:, CHANS : 2 * CHANS] + dot(sl[h], pt[h, :, 0:CHANS])

    def frequencies(c, out):
        parts = []
        for h in range(2):
            wide = dot(xt[h, c], sh[h])
            parts.append(wide[0:64] + wide[64:128] + dot(xt[h, c, 0:64, :], sl[h]))
        top = lax.broadcasted_iota(jnp.int32, (8, LEVELS * HALF), 0) < 4
        for j in range(CHIPS // 2):
            left, right = [part[8 * j : 8 * (j + 1)] for part in parts]
            out[2 * j] = jnp.where(top, left, right)
            out[2 * j + 1] = jnp.where(top, right, left)

    slopes(core)
    gi_own = increments_part(core)
    for b in range(BATCH):
        gi[b] = gi_own[b * STEPS : (b + 1) * STEPS]
    pair_coef.wait_recv()
    slopes(other)

    frequencies(other, gp_pair)
    pair_gp = remote(gp_pair, gp_in, pair_send.at[2], pair_recv.at[2], pair)
    pair_gp.start()
    frequencies(core, gp_own)
    gi_other = increments_part(other)
    for b in range(BATCH):
        gi[b] = gi[b] + gi_other[b * STEPS : (b + 1) * STEPS]
    z_copies = []
    for d in range(NZ - 1, 0, -1):
        k = z_at(d)
        src = gi.at[:, pl.ds(pl.multiple_of(k * PART, PART), PART), :]
        copy = remote(src, gi_in.at[z], z_send.at[k], z_recv.at[z], (tm, k))
        copy.start()
        z_copies.append(copy)
    pair_gp.wait_recv()
    gp_copies = []
    for d in range(1, CHIPS):
        k = chip_at(d)
        gp_own[k] = gp_own[k] + gp_in[k]
        copy = remote(gp_own.at[k], gp_recv.at[chip], u_send.at[k], u_recv.at[chip], (2 * k + core, z))
        copy.start()
        gp_copies.append(copy)
    gp_recv[chip] = gp_own[chip] + gp_in[chip]
    gi_in[z] = gi[:, pl.ds(pl.multiple_of(z * PART, PART), PART), :]

    for d in range(1, NZ):
        k = z_at(d)
        remote(gi_in.at[k], gi_in.at[k], z_send.at[k], z_recv.at[k], (tm, k)).wait_recv()
    total = gi_in[0]
    for k in range(1, NZ):
        total = total + gi_in[k]
    for b in range(BATCH):
        gi_out[pl.ds(b, PART, stride=BATCH), :] = total[b]

    for d in range(1, CHIPS):
        k = chip_at(d)
        remote(gp_recv.at[k], gp_recv.at[k], u_send.at[k], u_recv.at[k], (2 * k + core, z)).wait_recv()
    total = gp_recv[0]
    for k in range(1, CHIPS):
        total = total + gp_recv[k]
    swap = lax.rem(chip, 2)
    for m in range(LEVELS):
        lanes = slice(m * HALF, (m + 1) * HALF)
        gp_out[m, :, pl.ds(pl.multiple_of(swap * HALF, HALF), HALF)] = total[0:4, lanes]
        gp_out[m, :, pl.ds(pl.multiple_of((1 - swap) * HALF, HALF), HALF)] = total[4:8, lanes]
    for copy in [pair_summ, pair_coef, pair_gp] + chip_copies + z_copies + gp_copies:
        copy.wait_send()


def on_device(increments, projections, phases, groups):
    vmem = pl.BlockSpec(memory_space=pltpu.VMEM)
    hbm = pl.BlockSpec(memory_space=pl.ANY)
    dma = pltpu.SemaphoreType.DMA
    tile = (6, 8, 128)
    wide = LEVELS * HALF
    gi, gp = pl.pallas_call(
        kernel,
        out_shape=(
            jax.ShapeDtypeStruct((PART * BATCH, CHANS), F32),
            jax.ShapeDtypeStruct((LEVELS, CHANS // CHIPS // 2, WIDTH), F32),
        ),
        in_specs=[hbm, hbm, vmem, pl.BlockSpec(memory_space=pltpu.SMEM)],
        out_specs=(vmem, vmem),
        scratch_shapes=[
            pltpu.VMEM((ROWS, CHANS), F32),
            pltpu.VMEM((LEVELS, CHANS, WIDTH), F32),
            pltpu.VMEM((ROWS, 6 * CHANS), BF16),
            pltpu.VMEM((2, 2, CHANS, ROWS), BF16),
            pltpu.VMEM((LEVELS, 6 * CHANS, WIDTH), BF16),
            pltpu.VMEM((2, wide, 2 * CHANS), BF16),
            pltpu.VMEM((LEVELS, ROWS, WIDTH), F32),
            pltpu.VMEM((ROWS, WIDTH), F32),
            pltpu.VMEM((LEVELS, 2 * ROWS, WIDTH), BF16),
            pltpu.VMEM((6, ROWS, WIDTH), F32),
            pltpu.VMEM((2, ROWS, wide), BF16),
            pltpu.VMEM((2, ROWS, wide), BF16),
            pltpu.VMEM((2 * STEPS, 2 * STEPS), BF16),
            pltpu.VMEM((2, *tile), F32),
            pltpu.VMEM(tile, F32),
            pltpu.VMEM((CHIPS, *tile), F32),
            pltpu.VMEM((2, 5, 8, 128), F32),
            pltpu.VMEM((5, 8, 128), F32),
            pltpu.VMEM((CHIPS, 8, wide), F32),
            pltpu.VMEM((CHIPS, 8, wide), F32),
            pltpu.VMEM((CHIPS, 8, wide), F32),
            pltpu.VMEM((CHIPS, 8, wide), F32),
            pltpu.VMEM((BATCH, STEPS, CHANS), F32),
            pltpu.VMEM((NZ, BATCH, PART, CHANS), F32),
            dma((4,)),
            dma((3,)), dma((3,)),
            dma((CHIPS,)), dma((CHIPS,)),
            dma((CHIPS,)), dma((CHIPS,)),
            dma((NZ,)), dma((NZ,)),
        ],
        compiler_params=pltpu.CompilerParams(
            collective_id=0, has_side_effects=True, vmem_limit_bytes=60 << 20
        ),
    )(
        increments.reshape(ROWS, CHANS),
        projections.transpose(1, 0, 2),
        phases,
        groups,
    )
    return gi.reshape(PART, BATCH, CHANS), gp.transpose(1, 0, 2)


def solution(mesh):
    placed = (P("tm", None, None), P(None, None, "freq"), P(None, "freq"), P())
    return jax.shard_map(
        on_device,
        mesh=mesh,
        in_specs=placed,
        out_specs=(P(("tm", "freq"), None, None), P("tm", None, "freq")),
        check_vma=False,
    )
```

time: 428 us -> 35.9 us (0.08)
  blocking collectives: 188 us -> 0 us
  waiting for transfers between devices: 97.8 us -> 0 us
  matrix products: 69.5 us -> 0 us
  other arithmetic: 44.3 us -> 0 us
  Pallas kernels: 0 us -> 33 us
  between operations: 16.4 us -> 0.65 us
  local copies, waits for them, and re-layouts: 7.24 us -> 1.99 us
    all_gather x4 -> x0, blocking collectives: 124 us -> none  [prefix(): gathered = lax.all_gather(part, axis)]
    unnamed x3 -> x0, waiting for transfers between devices: 97.8 us -> none
    dot_general x13 -> x0, matrix products: 69.5 us -> none  [the longest x4 34.1 us: tiled_sum(): inner = jnp.einsum('ts,nsbf->ntbf', tri_mask, blocks, precision=highest)]
    psum x1 -> x0, blocking collectives: 64 us -> none  [global_gaps(): return lax.psum(stacked, 'tm')]
    add x63 -> x0, other arithmetic: 43.2 us -> none  [the longest x62 43.1 us: add_terms(): return early + late]
    pallas_call x0 -> x1, Pallas kernels: none -> 33 us  [on_device(): pl.pallas_call(kernel, out_shape=(jax.ShapeDtypeStruct((PART * BATCH, CHA...]
  transfers between devices with their start and end apart: 2 -> 0, of which waited for: 1 -> 0; matrix products, arithmetic and copies ran while one was open for 4% -> 0% of each run, Pallas kernels for 0% -> 0%
where the time goes in v2:
time: 35.9 us; the launch traced here: 35.7 us
  Pallas kernels  33 us (92%)
  local copies, waits for them, and re-layouts  1.99 us (6%)
  between operations  0.65 us (2%)
    pallas_call x1, Pallas kernels, on_device(): pl.pallas_call(kernel, out_shape=(jax.ShapeDtypeStruct((PART * BATCH, CHA...  33 us
    unnamed x4, local copies, waits for them, and re-layouts  1.99 us

profile of v2, /device:TPU:1, one launch (start us, length us, event | category | flops | bytes accessed | tf_op | source)
XLA Modules:
  0.0 35.7 jit_solution(2929460355534357070)
XLA Ops:
  0.6 33.0 %shard_map.59 = (f32[64,128]{1,0:T(8,128)}, f32[3,4,512]{2,1,0:T(4,128)}) custom-call(f32[512,128]{1,0:T(8,128)} %bitcast.5, f32[3,128,512]{2,1,0:T(8,128)} %bitcast.4, f32[3,512]{1,0:T(4,128)} %phase_ref.1, s32[4]{0:T(128)} %group_ref.1), custom_call_target="tpu_custom_call" | custom-call | tf_op jit(solution)/shard_map/pallas_call | solution.py:411
  33.7 0.0 copy-start
  33.7 1.4 %copy.8 = f32[16,4,128]{2,1,0:T(4,128)} copy(f32[16,4,128]{2,1,0:T(4,128)} %bitcast.6) | data formatting | bytes 65536
  35.1 0.0 copy-done
  35.1 0.6 %copy.9 = f32[4,3,512]{2,0,1:T(4,128)} copy(f32[4,3,512]{2,0,1:T(4,128)S(1)} %bitcast.7) | data formatting | bytes 49152
Async XLA Ops:
  33.7 1.4 %copy-start = (f32[3,4,512]{2,1,0:T(4,128)S(1)}, f32[3,4,512]{2,1,0:T(4,128)}, u32[]{:S(2)}) copy-start(f32[3,4,512]{2,1,0:T(4,128)} %get-tuple-element.5) | copy-start | bytes 73732

commit v3 on v2

--- a/solution.py
+++ b/solution.py
@@ -24,6 +24,14 @@
 ROWS = STEPS * BATCH
 PART = STEPS // NZ
 LEVELS = 3
+
+
+def ring(d, count):
+    return min(d, count - d)
+
+
+CHIP_ORDER = sorted(range(1, CHIPS), key=lambda d: -ring(d // NX, NY) - ring(d % NX, NX))
+Z_ORDER = sorted(range(1, NZ), key=lambda d: -ring(d, NZ))
 
 W0, W1, W2, A01, A12, A012 = range(6)
 
@@ -76,10 +84,10 @@
 
 
 def kernel(
-    inc_hbm, proj_hbm, phase_ref, group_ref, gi_out, gp_out,
-    inc_ref, proj_ref, xl, xt, pr, pt, fz, wb, whl, fb, sh, sl, tri,
-    summ, summ_in, chips, coef, coef_send, gp_pair, gp_own, gp_in, gp_recv, gi, gi_in,
-    in_sem, pair_send, pair_recv, c_send, c_recv, u_send, u_recv, z_send, z_recv,
+    inc_hbm, proj_hbm, phase_hbm, group_hbm, gi_out, gp_out,
+    inc_ref, proj_ref, phase_ref, group_ref, xl, xt, pr, pt, fz, wb, whl, fb, sh, sl, tri,
+    summ, summ_in, chips, coef, coef_send, gp_half, gp_pair, gp_own, gp_in, gp_recv, gi, gi_in,
+    in_sem, pair_send, pair_recv, g_send, g_recv, c_send, c_recv, u_send, u_recv, z_send, z_recv,
 ):
     amplitude = math.sqrt(2.0 / LENGTH)
     root = math.sqrt(2.0 * amplitude)
@@ -88,6 +96,8 @@
 
     loads = [pltpu.make_async_copy(inc_hbm, inc_ref, in_sem.at[0])]
     loads += [pltpu.make_async_copy(proj_hbm.at[m], proj_ref.at[m], in_sem.at[1 + m]) for m in range(LEVELS)]
+    loads.append(pltpu.make_async_copy(phase_hbm, phase_ref, in_sem.at[4]))
+    loads.append(pltpu.make_async_copy(group_hbm, group_ref, in_sem.at[5]))
     for load in loads:
         load.start()
 
@@ -97,13 +107,13 @@
     pair = (tm + 1 - 2 * core, z)
 
     def chip_at(d):
-        return lax.rem(chip + d, CHIPS)
+        return lax.rem(chip // NX + d // NX, NY) * NX + lax.rem(lax.rem(chip, NX) + d % NX, NX)
 
     def z_at(d):
         return lax.rem(z + d, NZ)
 
     barrier = pltpu.get_barrier_semaphore()
-    peers = [pair] + [(2 * chip_at(d) + core, z) for d in range(1, CHIPS)] + [(tm, z_at(d)) for d in range(1, NZ)]
+    peers = [pair] + [(2 * chip_at(d) + core, z) for d in CHIP_ORDER] + [(tm, z_at(d)) for d in range(1, NZ)]
     for peer in peers:
         pl.semaphore_signal(barrier, inc=1, device_id=peer, device_id_type=MESH)
 
@@ -146,6 +156,9 @@
             return carry
 
         lax.fori_loop(0, 2, split_projection, 0)
+
+    loads[4].wait()
+    loads[5].wait()
 
     pair_summ = remote(summ.at[other], summ_in, pair_send.at[0], pair_recv.at[0], pair)
 
@@ -209,7 +222,7 @@
     for q, tile in enumerate(join(core0, core1)):
         chips[chip, q] = tile
     chip_copies = []
-    for d in range(1, CHIPS):
+    for d in CHIP_ORDER:
         k = chip_at(d)
         copy = remote(chips.at[chip], chips.at[chip], c_send.at[k], c_recv.at[chip], (2 * k + core, z))
         copy.start()
@@ -269,7 +282,7 @@
         sign = jnp.where(group_ref[b] == 1, 2.0 / BATCH, -2.0 / BATCH).astype(F32)
         weight = jnp.where(lax.rem(sub, BATCH) == b, sign, weight)
 
-    for d in range(1, CHIPS):
+    for d in CHIP_ORDER:
         k = chip_at(d)
         remote(chips.at[k], chips.at[k], c_send.at[k], c_recv.at[k], (2 * k + core, z)).wait_recv()
     members = [[chips[k, q] for q in range(6)] for k in range(CHIPS)]
@@ -315,110 +328,121 @@
             at = pl.ds(pl.multiple_of(h * HALF + l * 128, 128), 128)
             for b in range(BATCH):
                 line = slice(l * BATCH + b, l * BATCH + b + 1)
-                c0, c1, s2, e1, e2 = [coef[h, k, line, :] for k in range(5)]
-                for t in range(0, STEPS, 64):
+                c0, c1, s2, e1, e2 = [jnp.broadcast_to(coef[h, k, line, :], (32, 128)) for k in range(5)]
+                for t in range(0, STEPS, 32):
                     r = b * STEPS + t
-                    here = slice(r, r + 64)
-                    b0, b1, a1, a2, b01, q = [fb[k, here, at] for k in range(6)]
-                    values = (
-                        fz[0, here, at] * (c0 + c1 * a1 + s2 * q),
-                        fz[1, here, at] * ((c1 + s2 * a2) * (e1 + b0)),
-                        fz[2, here, at] * (s2 * (e2 + e1 * b1 + b01)),
-                    )
-                    for m in range(LEVELS):
-                        high, low = halves(values[m])
+                    here = slice(r, r + 32)
+
+                    def keep(m, value):
+                        high, low = halves(value)
                         lanes = slice(m * HALF + l * 128, m * HALF + (l + 1) * 128)
                         sh[h, here, lanes] = high
                         sl[h, here, lanes] = low
 
+                    keep(0, fz[0, here, at] * (c0 + c1 * fb[2, here, at] + s2 * fb[5, here, at]))
+                    keep(1, fz[1, here, at] * ((c1 + s2 * fb[3, here, at]) * (e1 + fb[0, here, at])))
+                    keep(2, fz[2, here, at] * (s2 * (e2 + e1 * fb[1, here, at] + fb[4, here, at])))
+
     def increments_part(h):
         wide = dot(sh[h], pt[h])
         return wide[:, 0:CHANS] + wide[:, CHANS : 2 * CHANS] + dot(sl[h], pt[h, :, 0:CHANS])
 
-    def frequencies(c, out):
-        parts = []
-        for h in range(2):
-            wide = dot(xt[h, c], sh[h])
-            parts.append(wide[0:64] + wide[64:128] + dot(xt[h, c, 0:64, :], sl[h]))
-        top = lax.broadcasted_iota(jnp.int32, (8, LEVELS * HALF), 0) < 4
+    def frequencies_part(h, c):
+        wide = dot(xt[h, c], sh[h])
+        return wide[0:64] + wide[64:128] + dot(xt[h, c, 0:64, :], sl[h])
+
+    upper_rows = (lax.broadcasted_iota(jnp.int32, (8, LEVELS * HALF), 0) < 4).astype(F32)
+    ours = upper_rows * first + (1.0 - upper_rows) * (1.0 - first) > 0.5
+
+    def put_frequencies(slot, part, out):
         for j in range(CHIPS // 2):
-            left, right = [part[8 * j : 8 * (j + 1)] for part in parts]
-            out[2 * j] = jnp.where(top, left, right)
-            out[2 * j + 1] = jnp.where(top, right, left)
+            mine_rows, rest = gp_half[slot, 8 * j : 8 * (j + 1)], part[8 * j : 8 * (j + 1)]
+            out[2 * j] = jnp.where(ours, mine_rows, rest)
+            out[2 * j + 1] = jnp.where(ours, rest, mine_rows)
 
     slopes(core)
+    gp_half[0] = frequencies_part(core, other)
+    gp_half[1] = frequencies_part(core, core)
     gi_own = increments_part(core)
     for b in range(BATCH):
         gi[b] = gi_own[b * STEPS : (b + 1) * STEPS]
     pair_coef.wait_recv()
     slopes(other)
 
-    frequencies(other, gp_pair)
-    pair_gp = remote(gp_pair, gp_in, pair_send.at[2], pair_recv.at[2], pair)
-    pair_gp.start()
-    frequencies(core, gp_own)
+    put_frequencies(0, frequencies_part(other, other), gp_pair)
+    pair_copies = []
+    for d in CHIP_ORDER + [0]:
+        k = chip_at(d)
+        copy = remote(gp_pair.at[k], gp_in.at[k], g_send.at[k], g_recv.at[k], pair)
+        copy.start()
+        pair_copies.append(copy)
+    put_frequencies(1, frequencies_part(other, core), gp_own)
     gi_other = increments_part(other)
     for b in range(BATCH):
         gi[b] = gi[b] + gi_other[b * STEPS : (b + 1) * STEPS]
     z_copies = []
-    for d in range(NZ - 1, 0, -1):
+    for d in Z_ORDER:
         k = z_at(d)
         src = gi.at[:, pl.ds(pl.multiple_of(k * PART, PART), PART), :]
         copy = remote(src, gi_in.at[z], z_send.at[k], z_recv.at[z], (tm, k))
         copy.start()
         z_copies.append(copy)
-    pair_gp.wait_recv()
     gp_copies = []
-    for d in range(1, CHIPS):
+    for d, arrived in zip(CHIP_ORDER, pair_copies):
         k = chip_at(d)
+        arrived.wait_recv()
         gp_own[k] = gp_own[k] + gp_in[k]
         copy = remote(gp_own.at[k], gp_recv.at[chip], u_send.at[k], u_recv.at[chip], (2 * k + core, z))
         copy.start()
         gp_copies.append(copy)
+    pair_copies[-1].wait_recv()
     gp_recv[chip] = gp_own[chip] + gp_in[chip]
     gi_in[z] = gi[:, pl.ds(pl.multiple_of(z * PART, PART), PART), :]
 
-    for d in range(1, NZ):
+    for d in Z_ORDER:
         k = z_at(d)
         remote(gi_in.at[k], gi_in.at[k], z_send.at[k], z_recv.at[k], (tm, k)).wait_recv()
-    total = gi_in[0]
-    for k in range(1, NZ):
-        total = total + gi_in[k]
-    for b in range(BATCH):
-        gi_out[pl.ds(b, PART, stride=BATCH), :] = total[b]
-
-    for d in range(1, CHIPS):
+    for i in range(2):
+        total = gi_in[4 * i]
+        for k in range(4 * i + 1, 4 * (i + 1)):
+            total = total + gi_in[k]
+        for b in range(BATCH):
+            gi_out[i, pl.ds(b, PART, stride=BATCH), :] = total[b]
+
+    for d in CHIP_ORDER[::-1]:
         k = chip_at(d)
         remote(gp_recv.at[k], gp_recv.at[k], u_send.at[k], u_recv.at[k], (2 * k + core, z)).wait_recv()
-    total = gp_recv[0]
-    for k in range(1, CHIPS):
-        total = total + gp_recv[k]
     swap = lax.rem(chip, 2)
-    for m in range(LEVELS):
-        lanes = slice(m * HALF, (m + 1) * HALF)
-        gp_out[m, :, pl.ds(pl.multiple_of(swap * HALF, HALF), HALF)] = total[0:4, lanes]
-        gp_out[m, :, pl.ds(pl.multiple_of((1 - swap) * HALF, HALF), HALF)] = total[4:8, lanes]
-    for copy in [pair_summ, pair_coef, pair_gp] + chip_copies + z_copies + gp_copies:
+    for i in range(2):
+        total = gp_recv[8 * i]
+        for k in range(8 * i + 1, 8 * (i + 1)):
+            total = total + gp_recv[k]
+        for m in range(LEVELS):
+            lanes = slice(m * HALF, (m + 1) * HALF)
+            gp_out[i, m, :, pl.ds(pl.multiple_of(swap * HALF, HALF), HALF)] = total[0:4, lanes]
+            gp_out[i, m, :, pl.ds(pl.multiple_of((1 - swap) * HALF, HALF), HALF)] = total[4:8, lanes]
+    for copy in [pair_summ, pair_coef] + pair_copies + chip_copies + z_copies + gp_copies:
         copy.wait_send()
 
 
 def on_device(increments, projections, phases, groups):
-    vmem = pl.BlockSpec(memory_space=pltpu.VMEM)
-    hbm = pl.BlockSpec(memory_space=pl.ANY)
+    hbm = pl.BlockSpec(memory_space=pltpu.HBM)
     dma = pltpu.SemaphoreType.DMA
     tile = (6, 8, 128)
     wide = LEVELS * HALF
     gi, gp = pl.pallas_call(
         kernel,
         out_shape=(
-            jax.ShapeDtypeStruct((PART * BATCH, CHANS), F32),
-            jax.ShapeDtypeStruct((LEVELS, CHANS // CHIPS // 2, WIDTH), F32),
+            pltpu.VMEM((2, PART * BATCH, CHANS), F32),
+            pltpu.VMEM((2, LEVELS, CHANS // CHIPS // 2, WIDTH), F32),
         ),
-        in_specs=[hbm, hbm, vmem, pl.BlockSpec(memory_space=pltpu.SMEM)],
-        out_specs=(vmem, vmem),
+        in_specs=[hbm] * 4,
+        out_specs=(pl.BlockSpec(memory_space=pltpu.VMEM),) * 2,
         scratch_shapes=[
             pltpu.VMEM((ROWS, CHANS), F32),
             pltpu.VMEM((LEVELS, CHANS, WIDTH), F32),
+            pltpu.VMEM((LEVELS, WIDTH), F32),
+            pltpu.SMEM((BATCH,), jnp.int32),
             pltpu.VMEM((ROWS, 6 * CHANS), BF16),
             pltpu.VMEM((2, 2, CHANS, ROWS), BF16),
             pltpu.VMEM((LEVELS, 6 * CHANS, WIDTH), BF16),
@@ -435,14 +459,16 @@
             pltpu.VMEM((CHIPS, *tile), F32),
             pltpu.VMEM((2, 5, 8, 128), F32),
             pltpu.VMEM((5, 8, 128), F32),
+            pltpu.VMEM((2, 64, wide), F32),
             pltpu.VMEM((CHIPS, 8, wide), F32),
             pltpu.VMEM((CHIPS, 8, wide), F32),
             pltpu.VMEM((CHIPS, 8, wide), F32),
             pltpu.VMEM((CHIPS, 8, wide), F32),
             pltpu.VMEM((BATCH, STEPS, CHANS), F32),
             pltpu.VMEM((NZ, BATCH, PART, CHANS), F32),
-            dma((4,)),
-            dma((3,)), dma((3,)),
+            dma((6,)),
+            dma((2,)), dma((2,)),
+            dma((CHIPS,)), dma((CHIPS,)),
             dma((CHIPS,)), dma((CHIPS,)),
             dma((CHIPS,)), dma((CHIPS,)),
             dma((NZ,)), dma((NZ,)),
@@ -456,7 +482,7 @@
         phases,
         groups,
     )
-    return gi.reshape(PART, BATCH, CHANS), gp.transpose(1, 0, 2)
+    return (gi[0] + gi[1]).reshape(PART, BATCH, CHANS), (gp[0] + gp[1]).transpose(1, 0, 2)
 
 
 def solution(mesh):

time: 35.9 us -> 33.3 us (0.928)
  local copies, waits for them, and re-layouts: 1.99 us -> 0 us
  Pallas kernels: 33 us -> 31.3 us
  other arithmetic: 0 us -> 1.23 us
    unnamed x4 -> x0, local copies, waits for them, and re-layouts: 1.99 us -> none
    pallas_call x1, Pallas kernels: 33 us -> 31.3 us  [on_device(): pl.pallas_call(kernel, out_shape=(pltpu.VMEM((2, PART * BATCH, CHANS), F3...]
    add x0 -> x1, other arithmetic: none -> 0.62 us  [on_device(): gi[0] + gi[1]]
    transpose x0 -> x1, other arithmetic: none -> 0.61 us  [on_device(): (gp[0] + gp[1]).transpose(1, 0, 2)]
where the time goes in v3:
time: 33.3 us; the launch traced here: 33.2 us
  Pallas kernels  31.3 us (94%)
  other arithmetic  1.23 us (4%)
  between operations  0.64 us (2%)
    pallas_call x1, Pallas kernels, on_device(): pl.pallas_call(kernel, out_shape=(pltpu.VMEM((2, PART * BATCH, CHANS), F3...  31.3 us

profile of v3, /device:TPU:1, one launch (start us, length us, event | category | flops | bytes accessed | tf_op | source)
XLA Modules:
  0.0 33.2 jit_solution(13955949840343788005)
XLA Ops:
  0.6 31.3 %shard_map.59 = (f32[2,64,128]{2,1,0:T(8,128)S(1)}, f32[2,3,4,512]{3,2,1,0:T(4,128)S(1)}) custom-call(f32[512,128]{1,0:T(8,128)} %bitcast.8, f32[3,128,512]{2,1,0:T(8,128)} %bitcast.7, f32[3,512]{1,0:T(4,128)} %phase_hbm.1, s32[4]{0:T(128)} %group_hbm.1), custom_call_target="tpu_custom_call" | custom-call | tf_op jit(solution)/shard_map/pallas_call | solution.py:433
  32.0 0.6 %slice_add_fusion = f32[1,64,128]{2,1,0:T(8,128)} fusion(f32[2,64,128]{2,1,0:T(8,128)S(1)} %get-tuple-element.4), kind=kLoop, calls=%fused_computation | loop fusion | flops 8192 | bytes 98304 | tf_op jit(solution)/shard_map/add | solution.py:485
  32.6 0.6 %add_bitcast_fusion = f32[4,3,512]{2,0,1:T(4,128)} fusion(f32[2,3,4,512]{3,2,1,0:T(4,128)S(1)} %get-tuple-element.5), kind=kLoop, calls=%fused_computation.1 | loop fusion | flops 6144 | bytes 73728 | tf_op jit(solution)/shard_map/transpose | solution.py:485

commit v4 on v3

--- a/solution.py
+++ b/solution.py
@@ -376,7 +376,6 @@
         copy = remote(gp_pair.at[k], gp_in.at[k], g_send.at[k], g_recv.at[k], pair)
         copy.start()
         pair_copies.append(copy)
-    put_frequencies(1, frequencies_part(other, core), gp_own)
     gi_other = increments_part(other)
     for b in range(BATCH):
         gi[b] = gi[b] + gi_other[b * STEPS : (b + 1) * STEPS]
@@ -387,6 +386,7 @@
         copy = remote(src, gi_in.at[z], z_send.at[k], z_recv.at[z], (tm, k))
         copy.start()
         z_copies.append(copy)
+    put_frequencies(1, frequencies_part(other, core), gp_own)
     gp_copies = []
     for d, arrived in zip(CHIP_ORDER, pair_copies):
         k = chip_at(d)
@@ -402,27 +402,36 @@
     for d in Z_ORDER:
         k = z_at(d)
         remote(gi_in.at[k], gi_in.at[k], z_send.at[k], z_recv.at[k], (tm, k)).wait_recv()
-    for i in range(2):
-        total = gi_in[4 * i]
-        for k in range(4 * i + 1, 4 * (i + 1)):
-            total = total + gi_in[k]
-        for b in range(BATCH):
-            gi_out[i, pl.ds(b, PART, stride=BATCH), :] = total[b]
+    total = gi_in[0]
+    for k in range(1, NZ):
+        total = total + gi_in[k]
+    for b in range(BATCH):
+        gi_out[pl.ds(b, PART, stride=BATCH), :] = total[b]
 
     for d in CHIP_ORDER[::-1]:
         k = chip_at(d)
         remote(gp_recv.at[k], gp_recv.at[k], u_send.at[k], u_recv.at[k], (2 * k + core, z)).wait_recv()
     swap = lax.rem(chip, 2)
-    for i in range(2):
-        total = gp_recv[8 * i]
-        for k in range(8 * i + 1, 8 * (i + 1)):
-            total = total + gp_recv[k]
-        for m in range(LEVELS):
-            lanes = slice(m * HALF, (m + 1) * HALF)
-            gp_out[i, m, :, pl.ds(pl.multiple_of(swap * HALF, HALF), HALF)] = total[0:4, lanes]
-            gp_out[i, m, :, pl.ds(pl.multiple_of((1 - swap) * HALF, HALF), HALF)] = total[4:8, lanes]
+    total = gp_recv[0]
+    for k in range(1, CHIPS):
+        total = total + gp_recv[k]
+    for m in range(LEVELS):
+        lanes = slice(m * HALF, (m + 1) * HALF)
+        gp_out[m, :, pl.ds(pl.multiple_of(swap * HALF, HALF), HALF)] = total[0:4, lanes]
+        gp_out[m, :, pl.ds(pl.multiple_of((1 - swap) * HALF, HALF), HALF)] = total[4:8, lanes]
     for copy in [pair_summ, pair_coef] + pair_copies + chip_copies + z_copies + gp_copies:
         copy.wait_send()
+
+
+def store(gi_ref, gp_ref, gi_hbm, gp_hbm, sem):
+    copies = [
+        pltpu.make_async_copy(gi_ref, gi_hbm, sem.at[0]),
+        pltpu.make_async_copy(gp_ref, gp_hbm, sem.at[1]),
+    ]
+    for copy in copies:
+        copy.start()
+    for copy in copies:
+        copy.wait()
 
 
 def on_device(increments, projections, phases, groups):
@@ -430,14 +439,16 @@
     dma = pltpu.SemaphoreType.DMA
     tile = (6, 8, 128)
     wide = LEVELS * HALF
+    gi_shape, gp_shape = (PART * BATCH, CHANS), (LEVELS, CHANS // CHIPS // 2, WIDTH)
+    vmem = pl.BlockSpec(memory_space=pltpu.VMEM)
     gi, gp = pl.pallas_call(
         kernel,
         out_shape=(
-            pltpu.VMEM((2, PART * BATCH, CHANS), F32),
-            pltpu.VMEM((2, LEVELS, CHANS // CHIPS // 2, WIDTH), F32),
+            pltpu.VMEM(gi_shape, F32),
+            pltpu.VMEM(gp_shape, F32),
         ),
         in_specs=[hbm] * 4,
-        out_specs=(pl.BlockSpec(memory_space=pltpu.VMEM),) * 2,
+        out_specs=(vmem, vmem),
         scratch_shapes=[
             pltpu.VMEM((ROWS, CHANS), F32),
             pltpu.VMEM((LEVELS, CHANS, WIDTH), F32),
@@ -482,7 +493,15 @@
         phases,
         groups,
     )
-    return (gi[0] + gi[1]).reshape(PART, BATCH, CHANS), (gp[0] + gp[1]).transpose(1, 0, 2)
+    gi, gp = pl.pallas_call(
+        store,
+        out_shape=(jax.ShapeDtypeStruct(gi_shape, F32), jax.ShapeDtypeStruct(gp_shape, F32)),
+        in_specs=[vmem, vmem],
+        out_specs=(hbm, hbm),
+        scratch_shapes=[dma((2,))],
+        compiler_params=pltpu.CompilerParams(vmem_limit_bytes=1 << 20),
+    )(gi, gp)
+    return gi.reshape(PART, BATCH, CHANS), gp.transpose(1, 0, 2)
 
 
 def solution(mesh):

time: 33.3 us -> 32.9 us (0.988)
  other arithmetic: 1.23 us -> 0 us
  Pallas kernels: 31.3 us -> 32.1 us
    pallas_call x1 -> x2, Pallas kernels: 31.3 us -> 32.1 us  [the longest x1 31.5 us: on_device(): pl.pallas_call(kernel, out_shape=(pltpu.VMEM(gi_shape, F32), pltpu.VMEM(g...]
    add x1 -> x0, other arithmetic: 0.62 us -> none  [on_device(): gi[0] + gi[1]]
    transpose x1 -> x0, other arithmetic: 0.61 us -> none  [on_device(): (gp[0] + gp[1]).transpose(1, 0, 2)]
where the time goes in v4:
time: 32.9 us; the launch traced here: 32.8 us
  Pallas kernels  32.1 us (98%)
  between operations  0.64 us (2%)
    pallas_call x1, Pallas kernels, on_device(): pl.pallas_call(kernel, out_shape=(pltpu.VMEM(gi_shape, F32), pltpu.VMEM(g...  31.5 us

profile of v4, /device:TPU:1, one launch (start us, length us, event | category | flops | bytes accessed | tf_op | source)
XLA Modules:
  0.0 32.8 jit_solution(17522653287942545307)
XLA Ops:
  0.6 31.5 %shard_map.59 = (f32[64,128]{1,0:T(8,128)S(1)}, f32[3,4,512]{2,1,0:T(4,128)S(1)}) custom-call(f32[512,128]{1,0:T(8,128)} %bitcast.5, f32[3,128,512]{2,1,0:T(8,128)} %bitcast.4, f32[3,512]{1,0:T(4,128)} %phase_hbm.1, s32[4]{0:T(128)} %group_hbm.1), custom_call_target="tpu_custom_call" | custom-call | tf_op jit(solution)/shard_map/pallas_call | solution.py:444
  32.1 0.6 %shard_map.60 = (f32[64,128]{1,0:T(8,128)}, f32[3,4,512]{2,1,0:T(4,128)}) custom-call(f32[64,128]{1,0:T(8,128)S(1)} %get-tuple-element.6.gi_ref, f32[3,4,512]{2,1,0:T(4,128)S(1)} %get-tuple-element.7.gp_ref), custom_call_target="tpu_custom_call" | custom-call | tf_op jit(solution)/shard_map/pallas_call | solution.py:496

commit v5 on v4

--- a/solution.py
+++ b/solution.py
@@ -141,68 +141,87 @@
         for k, piece in enumerate((x1, x2, x1, x2, x3, x1)):
             xl[at, k * CHANS : (k + 1) * CHANS] = piece
 
-    for m in range(LEVELS):
-        loads[1 + m].wait()
-
-        def split_projection(i, carry, m=m):
-            at = pl.ds(pl.multiple_of(i * HALF, HALF), HALF)
-            block = proj_ref[m, :, at] * TURN
-            p1 = block.astype(BF16)
-            left = block - p1.astype(F32)
-            p2 = left.astype(BF16)
-            p3 = (left - p2.astype(F32)).astype(BF16)
-            for k, piece in enumerate((p1, p1, p2, p2, p1, p3)):
-                pr[m, k * CHANS : (k + 1) * CHANS, at] = piece
-            return carry
-
-        lax.fori_loop(0, 2, split_projection, 0)
+    for load in loads[1:4]:
+        load.wait()
+
+    def split_projection(m, h):
+        at = pl.ds(pl.multiple_of(h * HALF, HALF), HALF)
+        block = proj_ref[m, :, at] * TURN
+        p1 = block.astype(BF16)
+        left = block - p1.astype(F32)
+        p2 = left.astype(BF16)
+        p3 = (left - p2.astype(F32)).astype(BF16)
+        for k, piece in enumerate((p1, p1, p2, p2, p1, p3)):
+            pr[m, k * CHANS : (k + 1) * CHANS, at] = piece
 
     loads[4].wait()
     loads[5].wait()
 
     pair_summ = remote(summ.at[other], summ_in, pair_send.at[0], pair_recv.at[0], pair)
 
-    def local_sums(i, carry):
-        h = lax.rem(core + 1 + i, 2)
-        at = pl.ds(pl.multiple_of(h * HALF, HALF), HALF)
-
-        def put(q, b, total):
-            for l in range(2):
-                summ[h, q, l * BATCH + b : l * BATCH + b + 1, :] = total[:, l * 128 : (l + 1) * 128]
-
-        for m in range(LEVELS):
-            turns_all = dot(xl[...], pr[m, :, at])
-            shift = phase_ref[m : m + 1, at] * TURN
-            for b in range(BATCH):
-                total = jnp.zeros((16, HALF), F32)
-                for t in range(0, STEPS, 16):
-                    r = b * STEPS + t
-                    turns = turns_all[r : r + 16] + shift
-                    f = turns - jnp.round(turns)
-                    fz[m, r : r + 16, at] = f
-                    s = f * poly(sin_poly, f * f)
-                    w = amplitude - s * s
-                    total = total + w
-                    if m == 1:
-                        wb[r : r + 16, at] = w
+    def put(h, q, b, total):
+        for l in range(2):
+            summ[h, q, l * BATCH + b : l * BATCH + b + 1, :] = total[:, l * 128 : (l + 1) * 128]
+
+    def columns(h):
+        return pl.ds(pl.multiple_of(h * HALF, HALF), HALF)
+
+    def angles(m, h):
+        return dot(xl[...], pr[m, :, columns(h)])
+
+    def waves(m, h, turns_all):
+        at = columns(h)
+        shift = phase_ref[m : m + 1, at] * TURN
+        for b in range(BATCH):
+            total = jnp.zeros((16, HALF), F32)
+            for t in range(0, STEPS, 16):
+                r = b * STEPS + t
+                turns = turns_all[r : r + 16] + shift
+                f = turns - jnp.round(turns)
+                fz[m, r : r + 16, at] = f
+                s = f * poly(sin_poly, f * f)
+                w = amplitude - s * s
+                total = total + w
+                if m == 1:
+                    wb[r : r + 16, at] = w
+                else:
                     high, low = halves(w)
-                    whl[m, 2 * b * STEPS + t : 2 * b * STEPS + t + 16, at] = high
-                    whl[m, (2 * b + 1) * STEPS + t : (2 * b + 1) * STEPS + t + 16, at] = low
-                put(m, b, jnp.sum(total, axis=0, keepdims=True))
+                    whl[m // 2, 2 * b * STEPS + t : 2 * b * STEPS + t + 16, at] = high
+                    whl[m // 2, (2 * b + 1) * STEPS + t : (2 * b + 1) * STEPS + t + 16, at] = low
+            put(h, m, b, jnp.sum(total, axis=0, keepdims=True))
+
+    def local_scan(h, slot, level, row0):
+        at = columns(h)
         for b in range(BATCH):
-            here = slice(b * STEPS, (b + 1) * STEPS)
             both = slice(2 * b * STEPS, 2 * (b + 1) * STEPS)
-            b0 = dot(tri[0:STEPS, :], whl[0, both, at])
-            a2 = dot(tri[STEPS : 2 * STEPS, :], whl[2, both, at])
-            fb[0, here, at] = b0
-            fb[3, here, at] = a2
+            fb[slot, b * STEPS : (b + 1) * STEPS, at] = dot(tri[row0 : row0 + STEPS, :], whl[level, both, at])
+
+    def local_sums(h):
+        at = columns(h)
+        for b in range(BATCH):
             sums = [jnp.zeros((16, HALF), F32)] * 3
             for t in range(0, STEPS, 16):
-                w1 = wb[b * STEPS + t : b * STEPS + t + 16, at]
-                p, a = b0[t : t + 16] * w1, a2[t : t + 16]
+                r = b * STEPS + t
+                w1, a = wb[r : r + 16, at], fb[3, r : r + 16, at]
+                p = fb[0, r : r + 16, at] * w1
                 sums = [sums[0] + p, sums[1] + a * w1, sums[2] + a * p]
             for q, total in zip((A01, A12, A012), sums):
-                put(q, b, jnp.sum(total, axis=0, keepdims=True))
+                put(h, q, b, jnp.sum(total, axis=0, keepdims=True))
+
+    def half_sums(i, carry):
+        h = lax.rem(core + 1 + i, 2)
+        split_projection(0, h)
+        turns = angles(0, h)
+        split_projection(2, h)
+        later = angles(2, h)
+        split_projection(1, h)
+        waves(0, h, turns)
+        turns = angles(1, h)
+        waves(2, h, later)
+        local_scan(h, 0, 0, 0)
+        local_scan(h, 3, 1, STEPS)
+        waves(1, h, turns)
+        local_sums(h)
 
         @pl.when(i == 0)
         def _():
@@ -211,7 +230,7 @@
 
         return carry
 
-    lax.fori_loop(0, 2, local_sums, 0)
+    lax.fori_loop(0, 2, half_sums, 0)
 
     pair_summ.wait_recv()
     mine = [summ[core, q] for q in range(6)]
@@ -232,10 +251,10 @@
         at = pl.ds(pl.multiple_of(i * HALF, HALF), HALF)
         for b in range(BATCH):
             here = slice(b * STEPS, (b + 1) * STEPS)
-            both = dot(tri[...], whl[1, 2 * b * STEPS : 2 * (b + 1) * STEPS, at])
+            w1 = wb[here, at]
+            both = dot(tri[...], jnp.concatenate(halves(w1), axis=0))
             fb[1, here, at] = both[0:STEPS]
             fb[2, here, at] = both[STEPS : 2 * STEPS]
-            w1 = wb[here, at]
             fb[4, here, at] = dot(tri[0:STEPS, :], jnp.concatenate(halves(fb[0, here, at] * w1), axis=0))
             fb[5, here, at] = dot(tri[STEPS : 2 * STEPS, :], jnp.concatenate(halves(fb[3, here, at] * w1), axis=0))
         return carry
@@ -460,7 +479,7 @@
             pltpu.VMEM((2, wide, 2 * CHANS), BF16),
             pltpu.VMEM((LEVELS, ROWS, WIDTH), F32),
             pltpu.VMEM((ROWS, WIDTH), F32),
-            pltpu.VMEM((LEVELS, 2 * ROWS, WIDTH), BF16),
+            pltpu.VMEM((2, 2 * ROWS, WIDTH), BF16),
             pltpu.VMEM((6, ROWS, WIDTH), F32),
             pltpu.VMEM((2, ROWS, wide), BF16),
             pltpu.VMEM((2, ROWS, wide), BF16),

time: 32.9 us -> 32.8 us (level)
  no operation moved by 1% of the time
where the time goes in v5:
time: 32.8 us; the launch traced here: 32.7 us
  Pallas kernels  32.1 us (98%)
  between operations  0.64 us (2%)
    pallas_call x1, Pallas kernels, on_device(): pl.pallas_call(kernel, out_shape=(pltpu.VMEM(gi_shape, F32), pltpu.VMEM(g...  31.4 us

profile of v5, /device:TPU:1, one launch (start us, length us, event | category | flops | bytes accessed | tf_op | source)
XLA Modules:
  0.0 32.7 jit_solution(7425852517515294171)
XLA Ops:
  0.6 31.4 %shard_map.59 = (f32[64,128]{1,0:T(8,128)S(1)}, f32[3,4,512]{2,1,0:T(4,128)S(1)}) custom-call(f32[512,128]{1,0:T(8,128)} %bitcast.5, f32[3,128,512]{2,1,0:T(8,128)} %bitcast.4, f32[3,512]{1,0:T(4,128)} %phase_hbm.1, s32[4]{0:T(128)} %group_hbm.1), custom_call_target="tpu_custom_call" | custom-call | tf_op jit(solution)/shard_map/pallas_call | solution.py:463
  32.1 0.6 %shard_map.60 = (f32[64,128]{1,0:T(8,128)}, f32[3,4,512]{2,1,0:T(4,128)}) custom-call(f32[64,128]{1,0:T(8,128)S(1)} %get-tuple-element.6.gi_ref, f32[3,4,512]{2,1,0:T(4,128)S(1)} %get-tuple-element.7.gp_ref), custom_call_target="tpu_custom_call" | custom-call | tf_op jit(solution)/shard_map/pallas_call | solution.py:515
